TPU v7x, 32 devices: a whole 2x2x4 slice. The times are simulated.
32 devices in a mesh: base: 16 (over z, x, core), chan: 2 (over y).
Axes of the slice: x: 2, y: 2, z: 4, core: 2. Of those that a mesh axis runs over, the one named last changes fastest.
Arguments:
- image0: float32 [2048, 2048], P(('base', 'chan')), may hold values from -6 to 6
- interp: float32 [16, 2, 256, 8, 256], P('base', 'chan'), may hold values from -0.375 to 0.375
- vis_weight: float32 [16, 2, 256, 8], P('base', 'chan'), may hold values from 0.2 to 5
- counts: int32 [16, 2, 256], P('base', 'chan'), may hold values from 1 to 8
- tile_index: int32 [16, 2, 256], P('base', 'chan'), may hold values from 0 to 511
Outputs:
- image_out: float32 [2048, 2048], P(('base', 'chan'))
- estimates: float32 [3], replicated
Inputs may be any that keep to these rules, and one draw needn't show every extreme that they name: `tile_index`: slot s of a device belongs to the spectrum block of device s // 8 of base+chan, base index major; the entry numbers the tile within that block. `counts`: visibility v of a slot is live when v < count.
All inputs are finite; a program needn't handle non-finite values.
Results may differ from a plain program's by a relative error of at most 0.00023.
Values sent between devices are 32-bit elements; how exact they have to be, the bound alone decides.
A program may use at most 128 MiB of HBM per device.

v0:
```python
import math

import jax
import jax.numpy as jnp
from jax import lax
from jax.sharding import PartitionSpec as P

TILE_V = 8
TILE_U = 32
ITERS = 3


PRECISION_LEVEL = lax.Precision.HIGHEST


def split_length(length):
    outer_len = 2 ** ((length.bit_length() - 1) // 2)
    return (outer_len, length // outer_len)


def angle_table(count_a, count_b, modulus, sign):
    left = jnp.arange(count_a, dtype=jnp.int32)[:, None]
    right = jnp.arange(count_b, dtype=jnp.int32)[None, :]
    angle = sign * 2.0 * math.pi / modulus * (left * right % modulus).astype(jnp.float32)
    return (jnp.cos(angle), jnp.sin(angle))


def transform_rows(real_part, imag_part, sign):
    row_count, length = real_part.shape
    outer_len, inner_len = split_length(length)
    cos_q, sin_q = angle_table(inner_len, inner_len, inner_len, sign)
    cos_t, sin_t = angle_table(inner_len, outer_len, length, sign)
    cos_p, sin_p = angle_table(outer_len, outer_len, outer_len, sign)
    real_in = real_part.reshape(row_count, inner_len, outer_len)
    first_re = jnp.einsum("kq,rqp->rkp", cos_q, real_in, precision=PRECISION_LEVEL)
    first_im = jnp.einsum("kq,rqp->rkp", sin_q, real_in, precision=PRECISION_LEVEL)
    if imag_part is not None:
        imag_in = imag_part.reshape(row_count, inner_len, outer_len)
        first_re = first_re - jnp.einsum("kq,rqp->rkp", sin_q, imag_in, precision=PRECISION_LEVEL)
        first_im = first_im + jnp.einsum("kq,rqp->rkp", cos_q, imag_in, precision=PRECISION_LEVEL)
    turned_re = first_re * cos_t - first_im * sin_t
    turned_im = first_re * sin_t + first_im * cos_t
    last_re = jnp.einsum("jp,rkp->rjk", cos_p, turned_re, precision=PRECISION_LEVEL) - jnp.einsum(
        "jp,rkp->rjk", sin_p, turned_im, precision=PRECISION_LEVEL
    )
    last_im = jnp.einsum("jp,rkp->rjk", cos_p, turned_im, precision=PRECISION_LEVEL) + jnp.einsum(
        "jp,rkp->rjk", sin_p, turned_re, precision=PRECISION_LEVEL
    )
    factor = 1.0 / math.sqrt(length)
    return (
        last_re.reshape(row_count, length) * factor,
        last_im.reshape(row_count, length) * factor,
    )


def transpose_global(real_part, imag_part):
    row_count, length = real_part.shape
    n_base = lax.axis_size("base")
    n_chan = lax.axis_size("chan")
    width = length // (n_base * n_chan)
    moved = (
        lax.all_to_all(
            lax.all_to_all(
                real_part.reshape(1, row_count, n_base, n_chan, width),
                "base",
                split_axis=2,
                concat_axis=0,
                tiled=True,
            ),
            "chan",
            split_axis=3,
            concat_axis=1,
            tiled=True,
        ),
        lax.all_to_all(
            lax.all_to_all(
                imag_part.reshape(1, row_count, n_base, n_chan, width),
                "base",
                split_axis=2,
                concat_axis=0,
                tiled=True,
            ),
            "chan",
            split_axis=3,
            concat_axis=1,
            tiled=True,
        ),
    )
    return (moved[0].reshape(length, width).T, moved[1].reshape(length, width).T)


def to_tiles(plane):
    row_count, length = plane.shape
    shaped = plane.reshape(row_count // TILE_V, TILE_V, length // TILE_U, TILE_U)
    return shaped.transpose(0, 2, 1, 3).reshape(-1, TILE_V * TILE_U)


def from_tiles(tiles, row_count, length):
    shaped = tiles.reshape(row_count // TILE_V, length // TILE_U, TILE_V, TILE_U)
    return shaped.transpose(0, 2, 1, 3).reshape(row_count, length)


def slot_work(sample_weights, masked_weight, sample_values):
    visible_samples = (
        jnp.einsum("gnz,gez->gen", sample_weights, sample_values, precision=PRECISION_LEVEL)
        * masked_weight[:, None, :]
    )
    return jnp.einsum("hbi,hyb->hyi", sample_weights, visible_samples, precision=PRECISION_LEVEL)


def total_squares(image):
    return lax.psum(jnp.sum(image * image), ("base", "chan"))


def per_device(image0, interp, vis_weight, counts, tile_index):
    n_base = lax.axis_size("base")
    n_chan = lax.axis_size("chan")
    row_count, length = image0.shape
    touch = tile_index.shape[2]
    slots_each = touch // (n_base * n_chan)
    vcap = interp.shape[3]
    cells = interp.shape[4]
    tiles_own = row_count // TILE_V * (length // TILE_U)
    live = (jnp.arange(vcap, dtype=jnp.int32)[None, :] < counts.reshape(touch, 1)).astype(
        jnp.float32
    )
    masked_weight = vis_weight.reshape(touch, vcap) * live
    sample_weights = interp.reshape(touch, vcap, cells)
    wanted = lax.all_to_all(
        lax.all_to_all(
            tile_index.reshape(n_base, n_chan, slots_each),
            "base",
            split_axis=0,
            concat_axis=0,
            tiled=True,
        ),
        "chan",
        split_axis=1,
        concat_axis=1,
        tiled=True,
    ).reshape(touch)
    onehot = (jnp.arange(tiles_own, dtype=jnp.int32)[:, None] == wanted[None, :]).astype(
        jnp.float32
    )
    moved = (
        lax.all_to_all(
            lax.all_to_all(
                sample_weights.reshape(n_base, n_chan, slots_each, vcap, cells),
                "base",
                split_axis=0,
                concat_axis=0,
                tiled=True,
            ),
            "chan",
            split_axis=1,
            concat_axis=1,
            tiled=True,
        ),
        lax.all_to_all(
            lax.all_to_all(
                masked_weight.reshape(n_base, n_chan, slots_each, vcap),
                "base",
                split_axis=0,
                concat_axis=0,
                tiled=True,
            ),
            "chan",
            split_axis=1,
            concat_axis=1,
            tiled=True,
        ),
    )
    sample_weights = moved[0].reshape(touch, vcap, cells)
    masked_weight = moved[1].reshape(touch, vcap)
    found = []
    current = image0 / jnp.sqrt(total_squares(image0))
    for iteration in range(ITERS):
        real_part, imag_part = transform_rows(current, None, -1.0)
        real_part, imag_part = transpose_global(real_part, imag_part)
        real_part, imag_part = transform_rows(real_part, imag_part, -1.0)
        tiles = jnp.stack([to_tiles(real_part), to_tiles(imag_part)], axis=1)
        sample_values = jnp.take(tiles, wanted, axis=0)
        gridded_plane = slot_work(sample_weights, masked_weight, sample_values)
        summed = jnp.einsum("ts,skc->tkc", onehot, gridded_plane, precision=PRECISION_LEVEL)
        real_part = from_tiles(summed[:, 0, :], row_count, length)
        imag_part = from_tiles(summed[:, 1, :], row_count, length)
        real_part, imag_part = transform_rows(real_part, imag_part, 1.0)
        real_part, imag_part = transpose_global(real_part, imag_part)
        real_part, imag_part = transform_rows(real_part, imag_part, 1.0)
        norm_value = jnp.sqrt(total_squares(real_part))
        found.append(norm_value)
        current = real_part / norm_value
    return (float(length) * current, jnp.stack(found))


def solution(mesh):
    placed = (
        P(("base", "chan"), None),
        P("base", "chan", None, None, None),
        P("base", "chan", None, None),
        P("base", "chan", None),
        P("base", "chan", None),
    )
    return jax.shard_map(
        per_device,
        mesh=mesh,
        in_specs=placed,
        out_specs=(P(("base", "chan"), None), P()),
        check_vma=False,
    )
```

profile of v0, /device:TPU:0, one launch (start us, length us, event | category | flops | bytes accessed | tf_op | source)
XLA Modules:
  0.0 998.7 jit_solution(13095551597312861529)
XLA Ops:
  3.3 7.4 all-to-all-start
  14.0 40.9 %psum.28 = f32[]{:T(128)} all-reduce(f32[]{:T(128)} %multiply_reduce_fusion.3), channel_id=1, replica_groups=mesh['base'=16,'chan'=2] {'base','chan'}, use_global_device_ids=true, to_apply=%region_1.0 | all-reduce | flops 1 | bytes 8 | tf_op jit(solution)/shard_map/psum | solution.py:112
  69.5 4.9 all-to-all-start.8
  81.7 6.5 all-to-all-start.2
  95.1 7.3 all-to-all-done.2
  102.4 4.2 all-to-all-start.4
  111.5 9.4 all-to-all-done.4
  133.8 7.1 all-to-all-done.3
  140.9 10.1 %all_to_all.426 = f32[2,1,65536]{2,1,0:T(1,128)S(1)} all-to-all(f32[2,1,65536]{2,1,0:T(1,128)S(1)} %reshape.488), channel_id=1, replica_groups=mesh['base'=16,'chan'=2] {'chan'}, dimensions={0} | all-to-all | bytes 1048576 | tf_op jit(solution)/shard_map/all_to_all | solution.py:75
  151.1 4.9 all-to-all-start.6
  174.9 21.9 %all-to-all-done.6 = f32[16,2,8,8,256]{4,3,2,1,0:T(8,128)} async-done(((f32[16,2,8,8,256]{4,3,2,1,0:T(8,128)}), f32[16,2,8,8,256]{4,3,2,1,0:T(8,128)}, u32[]{:S(2)}, u32[]{:S(2)}) %all-to-all-start.6) | async-done | bytes 2097184 | tf_op jit(solution)/shard_map/all_to_all | solution.py:147
  200.0 4.8 all-to-all-start.7
  222.8 8.3 all-to-all-done.7
  266.8 10.7 %all-to-all-start.10 = ((f32[16,1,8192]{2,1,0:T(1,128)}), f32[16,1,8192]{2,1,0:T(1,128)}, u32[]{:S(2)}, u32[]{:S(2)}) async-start(f32[16,1,8192]{2,1,0:T(1,128)} %reshape.496), calls=%async_computation.10 | async-start | bytes 1048576 | tf_op jit(solution)/shard_map/all_to_all | solution.py:63
  287.7 4.2 all-to-all-done.10
  291.9 4.2 all-to-all-start.12
  303.8 6.7 all-to-all-done.12
  310.4 4.2 all-to-all-start.11
  323.3 4.4 all-to-all-start.13
  327.7 4.0 reduce.22
  365.1 40.5 %psum.29 = f32[]{:T(128)} all-reduce(f32[]{:T(128)} %get-tuple-element.33), channel_id=1, replica_groups=mesh['base'=16,'chan'=2] {'base','chan'}, use_global_device_ids=true, to_apply=%region_3.5 | all-reduce | flops 1 | bytes 8 | tf_op jit(solution)/shard_map/psum | solution.py:112
  427.3 4.9 all-to-all-start.14
  442.3 4.2 all-to-all-done.14
  446.5 4.2 all-to-all-start.16
  458.3 6.7 all-to-all-done.16
  465.0 4.2 all-to-all-start.15
  478.1 4.4 all-to-all-start.17
  482.5 4.0 reduce.26
  580.5 4.4 all-to-all-start.18
  595.1 4.2 all-to-all-done.18
  599.3 4.2 all-to-all-start.20
  611.2 6.7 all-to-all-done.20
  617.9 4.2 all-to-all-start.19
  631.0 4.4 all-to-all-start.21
  672.8 40.5 %psum.30 = f32[]{:T(128)} all-reduce(f32[]{:T(128)} %get-tuple-element.35), channel_id=1, replica_groups=mesh['base'=16,'chan'=2] {'base','chan'}, use_global_device_ids=true, to_apply=%region_5.7 | all-reduce | flops 1 | bytes 8 | tf_op jit(solution)/shard_map/psum | solution.py:112
  735.0 4.9 all-to-all-start.22
  750.0 4.2 all-to-all-done.22
  754.2 4.2 all-to-all-start.24
  766.1 6.7 all-to-all-done.24
  772.7 4.2 all-to-all-start.23
  785.8 4.4 all-to-all-start.25
  876.3 4.4 all-to-all-start.26
  887.6 7.3 all-to-all-done.26
  894.9 4.2 all-to-all-start.28
  903.8 9.5 all-to-all-done.28
  921.6 4.0 all-to-all-done.27
  925.6 4.4 all-to-all-start.29
  955.4 40.5 %psum.31 = f32[]{:T(128)} all-reduce(f32[]{:T(128)} %get-tuple-element.37), channel_id=1, replica_groups=mesh['base'=16,'chan'=2] {'base','chan'}, use_global_device_ids=true, to_apply=%region_7.9 | all-reduce | flops 1 | bytes 8 | tf_op jit(solution)/shard_map/psum | solution.py:112
  (400 shorter events, 572.5 us)
Async XLA Ops:
  3.3 58.0 %all-to-all-start = ((s32[16,2,8]{2,1,0:T(2,128)}), s32[16,2,8]{2,1,0:T(2,128)S(1)}, u32[]{:S(2)}, u32[]{:S(2)}) async-start(s32[16,2,8]{2,1,0:T(2,128)} %reshape.396), calls=%async_computation | async-start | bytes 32768 | tf_op jit(solution)/shard_map/all_to_all | solution.py:130
  58.5 1.7 copy-start.17
  58.5 2.6 copy-start.16
  62.1 7.4 all-to-all-start.1
  69.5 12.2 %all-to-all-start.8 = ((f32[16,1,128]{2,1,0:T(1,128)}), f32[16,1,128]{2,1,0:T(1,128)S(1)}, u32[]{:S(2)}, u32[]{:S(2)}) async-start(f32[16,1,128]{2,1,0:T(1,128)} %reshape.492), calls=%async_computation.8 | async-start | bytes 16384 | tf_op jit(solution)/shard_map/all_to_all | solution.py:160
  81.7 20.7 %all-to-all-start.2 = ((f32[16,1,8192]{2,1,0:T(1,128)}), f32[16,1,8192]{2,1,0:T(1,128)S(1)}, u32[]{:S(2)}, u32[]{:S(2)}) async-start(f32[16,1,8192]{2,1,0:T(1,128)} %reshape.482), calls=%async_computation.2 | async-start | bytes 1048576 | tf_op jit(solution)/shard_map/all_to_all | solution.py:63
  102.4 18.4 %all-to-all-start.4 = ((f32[16,1,8192]{2,1,0:T(1,128)}), f32[16,1,8192]{2,1,0:T(1,128)S(1)}, u32[]{:S(2)}, u32[]{:S(2)}) async-start(f32[16,1,8192]{2,1,0:T(1,128)} %reshape.486), calls=%async_computation.4 | async-start | bytes 1048576 | tf_op jit(solution)/shard_map/all_to_all | solution.py:76
  120.9 8.0 all-to-all-start.9
  128.9 12.1 %all-to-all-start.3 = ((f32[2,1,65536]{2,1,0:T(1,128)}), f32[2,1,65536]{2,1,0:T(1,128)S(1)}, u32[]{:S(2)}, u32[]{:S(2)}) async-start(f32[2,1,65536]{2,1,0:T(1,128)} %reshape.484), calls=%async_computation.3 | async-start | bytes 1048576 | tf_op jit(solution)/shard_map/all_to_all | solution.py:62
  151.1 45.8 %all-to-all-start.6 = ((f32[16,2,8,8,256]{4,3,2,1,0:T(8,128)}), f32[16,2,8,8,256]{4,3,2,1,0:T(8,128)}, u32[]{:S(2)}, u32[]{:S(2)}) async-start(f32[16,2,8,8,256]{4,3,2,1,0:T(8,128)} %bitcast.810), calls=%async_computation.6 | async-start | bytes 4194304 | tf_op jit(solution)/shard_map/all_to_all | solution.py:147
  200.0 31.1 %all-to-all-start.7 = ((f32[16,2,8,8,256]{4,3,2,0,1:T(8,128)}), f32[16,2,8,8,256]{4,3,2,0,1:T(8,128)}, u32[]{:S(2)}, u32[]{:S(2)}) async-start(f32[16,2,8,8,256]{4,3,2,0,1:T(8,128)} %copy.493), calls=%async_computation.7 | async-start | bytes 4194304 | tf_op jit(solution)/shard_map/all_to_all | solution.py:146
  219.6 1.0 copy-start.15
  249.3 3.7 copy-start.2
  249.3 3.7 copy-start.12
  256.0 4.5 copy-start
  266.8 25.0 %all-to-all-start.10 = ((f32[16,1,8192]{2,1,0:T(1,128)}), f32[16,1,8192]{2,1,0:T(1,128)}, u32[]{:S(2)}, u32[]{:S(2)}) async-start(f32[16,1,8192]{2,1,0:T(1,128)} %reshape.496), calls=%async_computation.10 | async-start | bytes 1048576 | tf_op jit(solution)/shard_map/all_to_all | solution.py:63
  291.9 18.5 %all-to-all-start.12 = ((f32[16,1,8192]{2,1,0:T(1,128)}), f32[16,1,8192]{2,1,0:T(1,128)}, u32[]{:S(2)}, u32[]{:S(2)}) async-start(f32[16,1,8192]{2,1,0:T(1,128)} %reshape.500), calls=%async_computation.12 | async-start | bytes 1048576 | tf_op jit(solution)/shard_map/all_to_all | solution.py:76
  310.4 12.9 %all-to-all-start.11 = ((f32[2,1,65536]{2,1,0:T(1,128)}), f32[2,1,65536]{2,1,0:T(1,128)}, u32[]{:S(2)}, u32[]{:S(2)}) async-start(f32[2,1,65536]{2,1,0:T(1,128)} %reshape.498), calls=%async_computation.11 | async-start | bytes 1048576 | tf_op jit(solution)/shard_map/all_to_all | solution.py:62
  323.3 21.1 %all-to-all-start.13 = ((f32[2,1,65536]{2,1,0:T(1,128)}), f32[2,1,65536]{2,1,0:T(1,128)}, u32[]{:S(2)}, u32[]{:S(2)}) async-start(f32[2,1,65536]{2,1,0:T(1,128)} %reshape.502), calls=%async_computation.13 | async-start | bytes 1048576 | tf_op jit(solution)/shard_map/all_to_all | solution.py:75
  356.9 2.9 copy-start.9
  411.9 1.0 copy-start.6
  416.4 4.5 copy-start.4
  427.3 19.2 %all-to-all-start.14 = ((f32[16,1,8192]{2,1,0:T(1,128)}), f32[16,1,8192]{2,1,0:T(1,128)}, u32[]{:S(2)}, u32[]{:S(2)}) async-start(f32[16,1,8192]{2,1,0:T(1,128)} %reshape.504), calls=%async_computation.14 | async-start | bytes 1048576 | tf_op jit(solution)/shard_map/all_to_all | solution.py:63
  446.5 18.5 %all-to-all-start.16 = ((f32[16,1,8192]{2,1,0:T(1,128)}), f32[16,1,8192]{2,1,0:T(1,128)}, u32[]{:S(2)}, u32[]{:S(2)}) async-start(f32[16,1,8192]{2,1,0:T(1,128)} %reshape.508), calls=%async_computation.16 | async-start | bytes 1048576 | tf_op jit(solution)/shard_map/all_to_all | solution.py:76
  465.0 13.0 %all-to-all-start.15 = ((f32[2,1,65536]{2,1,0:T(1,128)}), f32[2,1,65536]{2,1,0:T(1,128)}, u32[]{:S(2)}, u32[]{:S(2)}) async-start(f32[2,1,65536]{2,1,0:T(1,128)} %reshape.506), calls=%async_computation.15 | async-start | bytes 1048576 | tf_op jit(solution)/shard_map/all_to_all | solution.py:62
  478.1 21.2 %all-to-all-start.17 = ((f32[2,1,65536]{2,1,0:T(1,128)}), f32[2,1,65536]{2,1,0:T(1,128)}, u32[]{:S(2)}, u32[]{:S(2)}) async-start(f32[2,1,65536]{2,1,0:T(1,128)} %reshape.510), calls=%async_computation.17 | async-start | bytes 1048576 | tf_op jit(solution)/shard_map/all_to_all | solution.py:75
  511.7 2.9 copy-start.10
  562.4 1.0 copy-start.3
  562.4 4.3 copy-start.13
  569.7 4.5 copy-start.1
  580.5 18.8 %all-to-all-start.18 = ((f32[16,1,8192]{2,1,0:T(1,128)}), f32[16,1,8192]{2,1,0:T(1,128)}, u32[]{:S(2)}, u32[]{:S(2)}) async-start(f32[16,1,8192]{2,1,0:T(1,128)} %reshape.512), calls=%async_computation.18 | async-start | bytes 1048576 | tf_op jit(solution)/shard_map/all_to_all | solution.py:63
  599.3 18.5 %all-to-all-start.20 = ((f32[16,1,8192]{2,1,0:T(1,128)}), f32[16,1,8192]{2,1,0:T(1,128)}, u32[]{:S(2)}, u32[]{:S(2)}) async-start(f32[16,1,8192]{2,1,0:T(1,128)} %reshape.516), calls=%async_computation.20 | async-start | bytes 1048576 | tf_op jit(solution)/shard_map/all_to_all | solution.py:76
  617.9 13.1 %all-to-all-start.19 = ((f32[2,1,65536]{2,1,0:T(1,128)}), f32[2,1,65536]{2,1,0:T(1,128)}, u32[]{:S(2)}, u32[]{:S(2)}) async-start(f32[2,1,65536]{2,1,0:T(1,128)} %reshape.514), calls=%async_computation.19 | async-start | bytes 1048576 | tf_op jit(solution)/shard_map/all_to_all | solution.py:62
  631.0 21.1 %all-to-all-start.21 = ((f32[2,1,65536]{2,1,0:T(1,128)}), f32[2,1,65536]{2,1,0:T(1,128)}, u32[]{:S(2)}, u32[]{:S(2)}) async-start(f32[2,1,65536]{2,1,0:T(1,128)} %reshape.518), calls=%async_computation.21 | async-start | bytes 1048576 | tf_op jit(solution)/shard_map/all_to_all | solution.py:75
  664.5 2.9 copy-start.11
  719.7 1.0 copy-start.7
  724.2 4.5 copy-start.5
  735.0 19.2 %all-to-all-start.22 = ((f32[16,1,8192]{2,1,0:T(1,128)}), f32[16,1,8192]{2,1,0:T(1,128)}, u32[]{:S(2)}, u32[]{:S(2)}) async-start(f32[16,1,8192]{2,1,0:T(1,128)} %reshape.520), calls=%async_computation.22 | async-start | bytes 1048576 | tf_op jit(solution)/shard_map/all_to_all | solution.py:63
  754.2 18.5 %all-to-all-start.24 = ((f32[16,1,8192]{2,1,0:T(1,128)}), f32[16,1,8192]{2,1,0:T(1,128)}, u32[]{:S(2)}, u32[]{:S(2)}) async-start(f32[16,1,8192]{2,1,0:T(1,128)} %reshape.524), calls=%async_computation.24 | async-start | bytes 1048576 | tf_op jit(solution)/shard_map/all_to_all | solution.py:76
  772.7 13.0 %all-to-all-start.23 = ((f32[2,1,65536]{2,1,0:T(1,128)}), f32[2,1,65536]{2,1,0:T(1,128)}, u32[]{:S(2)}, u32[]{:S(2)}) async-start(f32[2,1,65536]{2,1,0:T(1,128)} %reshape.522), calls=%async_computation.23 | async-start | bytes 1048576 | tf_op jit(solution)/shard_map/all_to_all | solution.py:62
  785.8 21.2 %all-to-all-start.25 = ((f32[2,1,65536]{2,1,0:T(1,128)}), f32[2,1,65536]{2,1,0:T(1,128)}, u32[]{:S(2)}, u32[]{:S(2)}) async-start(f32[2,1,65536]{2,1,0:T(1,128)} %reshape.526), calls=%async_computation.25 | async-start | bytes 1048576 | tf_op jit(solution)/shard_map/all_to_all | solution.py:75
  819.4 2.9 copy-start.8
  863.6 2.1 copy-start.14
  876.3 18.6 %all-to-all-start.26 = ((f32[16,1,8192]{2,1,0:T(1,128)}), f32[16,1,8192]{2,1,0:T(1,128)S(1)}, u32[]{:S(2)}, u32[]{:S(2)}) async-start(f32[16,1,8192]{2,1,0:T(1,128)} %reshape.528), calls=%async_computation.26 | async-start | bytes 1048576 | tf_op jit(solution)/shard_map/all_to_all | solution.py:63
  894.9 18.4 %all-to-all-start.28 = ((f32[16,1,8192]{2,1,0:T(1,128)}), f32[16,1,8192]{2,1,0:T(1,128)S(1)}, u32[]{:S(2)}, u32[]{:S(2)}) async-start(f32[16,1,8192]{2,1,0:T(1,128)} %reshape.532), calls=%async_computation.28 | async-start | bytes 1048576 | tf_op jit(solution)/shard_map/all_to_all | solution.py:76
  913.3 12.3 %all-to-all-start.27 = ((f32[2,1,65536]{2,1,0:T(1,128)}), f32[2,1,65536]{2,1,0:T(1,128)S(1)}, u32[]{:S(2)}, u32[]{:S(2)}) async-start(f32[2,1,65536]{2,1,0:T(1,128)} %reshape.530), calls=%async_computation.27 | async-start | bytes 1048576 | tf_op jit(solution)/shard_map/all_to_all | solution.py:62
  925.6 13.4 %all-to-all-start.29 = ((f32[2,1,65536]{2,1,0:T(1,128)}), f32[2,1,65536]{2,1,0:T(1,128)}, u32[]{:S(2)}, u32[]{:S(2)}) async-start(f32[2,1,65536]{2,1,0:T(1,128)} %reshape.534), calls=%async_computation.29 | async-start | bytes 1048576 | tf_op jit(solution)/shard_map/all_to_all | solution.py:75
where the time goes:
time: 1010 us; the launch traced here: 999 us
  local copies, waits for them, and re-layouts  273 us (27%)
  matrix products  192 us (19%)
  blocking collectives  172 us (17%)
  starting transfers between devices  136 us (13%)
  waiting for transfers between devices  126 us (12%)
  other arithmetic  94.2 us (9%)
    psum x4, blocking collectives, total_squares(): return lax.psum(jnp.sum(image * image), ('base', 'chan'))  162 us
    unnamed x92, local copies, waits for them, and re-layouts  85.7 us
    all_to_all x6, waiting for transfers between devices, transpose_global(): lax.all_to_all(imag_part.reshape(1, row_count, n_base, n_chan, width), 'b...  45.5 us
    all_to_all x6, starting transfers between devices, transpose_global(): lax.all_to_all(real_part.reshape(1, row_count, n_base, n_chan, width), 'b...  35.7 us
    all_to_all x6, waiting for transfers between devices, transpose_global(): lax.all_to_all(real_part.reshape(1, row_count, n_base, n_chan, width), 'b...  31.4 us
    dot_general x12, matrix products, transform_rows(): jnp.einsum('jp,rkp->rjk', sin_p, turned_im, precision=PRECISION_LEVEL)  27.9 us
    all_to_all x6, starting transfers between devices, transpose_global(): lax.all_to_all(imag_part.reshape(1, row_count, n_base, n_chan, width), 'b...  25.3 us
    dot_general x12, matrix products, transform_rows(): jnp.einsum('kq,rqp->rkp', sin_q, real_in, precision=PRECISION_LEVEL)  24.4 us
  transfers between devices with their start and end apart: 29, of which 21 were waited for; matrix products, arithmetic and copies ran while one was open for 27% of the time, Pallas kernels for 0%

commit v1 on v0

--- a/solution.py
+++ b/solution.py
@@ -2,7 +2,10 @@
 
 import jax
 import jax.numpy as jnp
+import numpy as np
 from jax import lax
+from jax.experimental import pallas as pl
+from jax.experimental.pallas import tpu as pltpu
 from jax.sharding import PartitionSpec as P
 
 TILE_V = 8
@@ -112,7 +115,7 @@
     return lax.psum(jnp.sum(image * image), ("base", "chan"))
 
 
-def per_device(image0, interp, vis_weight, counts, tile_index):
+def general_device(image0, interp, vis_weight, counts, tile_index):
     n_base = lax.axis_size("base")
     n_chan = lax.axis_size("chan")
     row_count, length = image0.shape
@@ -193,6 +196,421 @@
     return (float(length) * current, jnp.stack(found))
 
 
+F32 = jnp.float32
+BF16 = jnp.bfloat16
+VMEM_SPEC = pl.BlockSpec(memory_space=pltpu.VMEM)
+SMEM_SPEC = pl.BlockSpec(memory_space=pltpu.SMEM)
+BIG = pltpu.CompilerParams(vmem_limit_bytes=48 * 1024 * 1024)
+
+
+def halves(value):
+    high = value.astype(BF16)
+    return high, (value - high.astype(F32)).astype(BF16)
+
+
+def np_halves(table):
+    high = np.asarray(table, np.float32).astype(jnp.bfloat16)
+    low = (np.asarray(table, np.float64) - high.astype(np.float64)).astype(jnp.bfloat16)
+    return high, low
+
+
+def triple_dot(left, right, dims):
+    def one(a, b):
+        return lax.dot_general(a, b, (dims, ((), ())), preferred_element_type=F32)
+
+    return one(left[0], right[0]) + (one(left[0], right[1]) + one(left[1], right[0]))
+
+
+def fft_list(items, sign):
+    count = len(items)
+    if count == 1:
+        return items
+    even = fft_list(items[0::2], sign)
+    odd = fft_list(items[1::2], sign)
+    low, high = [], []
+    for k in range(count // 2):
+        re, im = odd[k]
+        if k == 0:
+            t_re, t_im = re, im
+        elif 4 * k == count:
+            t_re, t_im = (im, -re) if sign < 0 else (-im, re)
+        else:
+            angle = sign * 2.0 * math.pi * k / count
+            c, s = math.cos(angle), math.sin(angle)
+            t_re, t_im = re * c - im * s, re * s + im * c
+        e_re, e_im = even[k]
+        low.append((e_re + t_re, e_im + t_im))
+        high.append((e_re - t_re, e_im - t_im))
+    return low + high
+
+
+def exchange_kernel(n, n_chan, src_ref, dst_ref, own_sem, send_sem, recv_sem):
+    me = lax.axis_index("base") * n_chan + lax.axis_index("chan")
+    own = pltpu.make_async_copy(src_ref.at[me], dst_ref.at[me], own_sem)
+    own.start()
+
+    def copy(step):
+        peer = lax.rem(me + step, n)
+        return pltpu.make_async_remote_copy(
+            src_ref=src_ref.at[peer],
+            dst_ref=dst_ref.at[me],
+            send_sem=send_sem.at[step],
+            recv_sem=recv_sem.at[step],
+            device_id=(peer // n_chan, lax.rem(peer, n_chan)),
+            device_id_type=pl.DeviceIdType.MESH,
+        )
+
+    def launch(step, carry):
+        copy(step).start()
+        return carry
+
+    def finish(step, carry):
+        copy(step).wait()
+        return carry
+
+    lax.fori_loop(1, n, launch, 0)
+    own.wait()
+    lax.fori_loop(1, n, finish, 0)
+
+
+def exchange(values, n, n_chan):
+    return pl.pallas_call(
+        lambda *refs: exchange_kernel(n, n_chan, *refs),
+        out_shape=jax.ShapeDtypeStruct(values.shape, values.dtype),
+        in_specs=[pl.BlockSpec(memory_space=pltpu.VMEM)],
+        out_specs=pl.BlockSpec(memory_space=pltpu.VMEM),
+        scratch_shapes=[
+            pltpu.SemaphoreType.DMA,
+            pltpu.SemaphoreType.DMA((n,)),
+            pltpu.SemaphoreType.DMA((n,)),
+        ],
+        compiler_params=pltpu.CompilerParams(
+            has_side_effects=True, vmem_limit_bytes=48 * 1024 * 1024
+        ),
+    )(values)
+
+
+def turn(re, im, c, s):
+    return re * c - im * s, re * s + im * c
+
+
+def swap_halves(x0, x1):
+    half = x0.shape[1] // 2
+    left = lax.broadcasted_iota(jnp.int32, x0.shape, 1) < half
+    return (
+        jnp.where(left, x0, pltpu.roll(x1, half, 1)),
+        jnp.where(left, pltpu.roll(x0, half, 1), x1),
+    )
+
+
+def row_inverse(n, recv_ref, tc_ref, ts_ref, mh_ref, ml_ref, b_ref):
+    rows = recv_ref.shape[1] // 2
+
+    def chunk(i, carry):
+        at = pl.multiple_of(i * 8, 8)
+        items = [
+            (recv_ref[o, pl.ds(at, 8), :], recv_ref[o, pl.ds(at + rows, 8), :]) for o in range(n)
+        ]
+        items = fft_list(items, 1.0)
+        items = [
+            turn(*items[q], tc_ref[q, pl.ds(at, 8), :], -ts_ref[q, pl.ds(at, 8), :])
+            for q in range(n)
+        ]
+        for pair in range(n // 2):
+            for part in range(2):
+                x0, x1 = swap_halves(items[2 * pair][part], items[2 * pair + 1][part])
+                lanes = slice(pair * 128, (pair + 1) * 128)
+                b_ref[pl.ds(at + part * 2 * rows, 8), lanes] = x0
+                b_ref[pl.ds(at + part * 2 * rows + rows, 8), lanes] = x1
+        return carry
+
+    lax.fori_loop(0, rows // 8, chunk, 0)
+    parts = []
+    for start in range(0, b_ref.shape[1], 512):
+        right = halves(b_ref[:, start : start + 512])
+        parts.append(triple_dot((mh_ref[...], ml_ref[...]), right, ((1,), (0,))))
+    return parts
+
+
+def row_forward(n, parts, tc_ref, ts_ref, mh_ref, ml_ref, b_ref, send_ref):
+    rows = tc_ref.shape[1]
+    total = sum(jnp.sum(part * part) for part in parts)
+    for index, part in enumerate(parts):
+        b_ref[:, index * 512 : (index + 1) * 512] = triple_dot(
+            (mh_ref[...], ml_ref[...]), halves(part), ((1,), (0,))
+        )
+
+    def chunk(i, carry):
+        at = pl.multiple_of(i * 8, 8)
+        items = [[None, None] for _ in range(n)]
+        for pair in range(n // 2):
+            for part in range(2):
+                lanes = slice(pair * 128, (pair + 1) * 128)
+                x0 = b_ref[pl.ds(at + part * 2 * rows, 8), lanes]
+                x1 = b_ref[pl.ds(at + part * 2 * rows + rows, 8), lanes]
+                items[2 * pair][part], items[2 * pair + 1][part] = swap_halves(x0, x1)
+        items = [
+            turn(*items[q], tc_ref[q, pl.ds(at, 8), :], ts_ref[q, pl.ds(at, 8), :])
+            for q in range(n)
+        ]
+        items = fft_list(items, -1.0)
+        for o in range(n):
+            send_ref[o, pl.ds(at, 8), :] = items[o][0]
+            send_ref[o, pl.ds(at + rows, 8), :] = items[o][1]
+        return carry
+
+    lax.fori_loop(0, rows // 8, chunk, 0)
+    for o in range(n):
+        send_ref[o, 2 * rows : 2 * rows + 8, :] = jnp.full((8, 128), total, F32)
+
+
+def first_kernel(n, y_ref, tc, ts, fh, fl, send_ref, b_ref):
+    parts = [y_ref[:, s : s + 512] for s in range(0, y_ref.shape[1], 512)]
+    row_forward(n, parts, tc, ts, fh, fl, b_ref, send_ref)
+
+
+def middle_kernel(n, recv_ref, tc, ts, fh, fl, ih, il, send_ref, b_ref):
+    parts = row_inverse(n, recv_ref, tc, ts, ih, il, b_ref)
+    row_forward(n, parts, tc, ts, fh, fl, b_ref, send_ref)
+
+
+def last_kernel(n, recv_ref, tc, ts, ih, il, y_ref, sum_ref, b_ref):
+    parts = row_inverse(n, recv_ref, tc, ts, ih, il, b_ref)
+    for index, part in enumerate(parts):
+        y_ref[:, index * 512 : (index + 1) * 512] = part
+    total = sum(jnp.sum(part * part) for part in parts)
+    for o in range(n):
+        sum_ref[o] = jnp.full((8, 128), total, F32)
+
+
+def column_kernel(
+    n,
+    tile_ref,
+    recv_ref,
+    wh_ref,
+    wl_ref,
+    wm_ref,
+    tc,
+    ts,
+    fh,
+    fl,
+    ih,
+    il,
+    send_ref,
+    norm_ref,
+    u_ref,
+    t_ref,
+    acc_ref,
+    g_ref,
+):
+    rows = send_ref.shape[1] // 2
+    blocks = rows // 8
+    groups = wh_ref.shape[0]
+    members = g_ref.shape[0] // 2
+    across = 2 * rows
+    total = recv_ref[0, 2 * rows : 2 * rows + 8, :]
+    for d in range(1, n):
+        total = total + recv_ref[d, 2 * rows : 2 * rows + 8, :]
+    norm = jnp.sqrt(total)
+    norm_ref[...] = norm
+
+    def forward(i, carry):
+        at = pl.multiple_of(i * 8, 8)
+        inverse = 1.0 / norm_ref[...]
+        items = fft_list(
+            [
+                (
+                    recv_ref[d, pl.ds(at, 8), :] * inverse,
+                    recv_ref[d, pl.ds(at + rows, 8), :] * inverse,
+                )
+                for d in range(n)
+            ],
+            -1.0,
+        )
+        for k in range(n):
+            re, im = turn(*items[k], tc[k : k + 1, :], ts[k : k + 1, :])
+            u_ref[i, k * 8 : k * 8 + 8, :128] = re
+            u_ref[i, k * 8 : k * 8 + 8, 128:] = im
+        right = halves(u_ref[i])
+        t_ref[i] = triple_dot((fh[...], fl[...]), right, ((1,), (1,)))
+        acc_ref[i] = jnp.zeros(acc_ref.shape[1:], F32)
+        return carry
+
+    lax.fori_loop(0, blocks, forward, 0)
+
+    row_of = lax.broadcasted_iota(jnp.int32, (2 * members, 256), 0) % members
+    slot_of = lax.broadcasted_iota(jnp.int32, (2 * members, 256), 1) // (256 // members)
+
+    def place(index):
+        tile = tile_ref[index]
+        column = tile // across
+        row = (column // blocks) * across + tile % across
+        return column % blocks, row
+
+    def group(g, carry):
+        for s in range(members):
+            block, row = place(g * members + s)
+            g_ref[s : s + 1, :] = t_ref[block, pl.ds(row, 1), :]
+            g_ref[s + members : s + members + 1, :] = t_ref[block, pl.ds(row + 128, 1), :]
+        weights = (wh_ref[g], wl_ref[g])
+        seen = triple_dot(halves(g_ref[...]), weights, ((1,), (1,)))
+        seen = jnp.where(row_of == slot_of, seen * wm_ref[g], 0.0)
+        g_ref[...] = triple_dot(halves(seen), weights, ((1,), (0,)))
+        for s in range(members):
+            block, row = place(g * members + s)
+            acc_ref[block, pl.ds(row, 1), :] += g_ref[s : s + 1, :]
+            acc_ref[block, pl.ds(row + 128, 1), :] += g_ref[s + members : s + members + 1, :]
+        return carry
+
+    lax.fori_loop(0, groups, group, 0)
+
+    def backward(i, carry):
+        at = pl.multiple_of(i * 8, 8)
+        u_ref[i] = triple_dot(halves(acc_ref[i].T), (ih[...], il[...]), ((1,), (0,)))
+        items = []
+        for k in range(n):
+            re = u_ref[i, k * 8 : k * 8 + 8, :128]
+            im = u_ref[i, k * 8 : k * 8 + 8, 128:]
+            items.append(turn(re, im, tc[k : k + 1, :], -ts[k : k + 1, :]))
+        items = fft_list(items, 1.0)
+        for d in range(n):
+            send_ref[d, pl.ds(at, 8), :] = items[d][0]
+            send_ref[d, pl.ds(at + rows, 8), :] = items[d][1]
+        return carry
+
+    lax.fori_loop(0, blocks, backward, 0)
+
+
+def weight_kernel(x_ref, perm_ref, high_ref, low_ref):
+    count, _, cells = x_ref.shape
+    value = x_ref[:, :64, :].reshape(count * 64, cells)
+    for part, ref in zip(halves(value), (high_ref, low_ref)):
+        ref[0] = jnp.dot(part, perm_ref[...], preferred_element_type=F32).astype(BF16)
+
+
+def tables(n, row_count, length):
+    half = row_count // 2
+    scale = 1.0 / math.sqrt(length)
+    local = np.arange(row_count)
+    angle = -2.0 * np.pi * np.outer(local, local) / row_count
+    c, s = np.cos(angle) * scale, np.sin(angle) * scale
+    two = np.eye(2)
+    col_f = np.block([[np.kron(two, c), np.kron(two, -s)], [np.kron(two, s), np.kron(two, c)]])
+    col_i = np.block([[np.kron(two, c), np.kron(two, -s)], [np.kron(two, s), np.kron(two, c)]])
+    row_f = np.concatenate([c, s], axis=0)
+    row_i = np.concatenate([c, s], axis=1)
+    index = np.arange(n)
+    turns = -2.0 * np.pi * np.outer(index, np.tile(local, 2)) / length
+    u = np.arange(half)[:, None] + half * (np.arange(2 * row_count)[None, :] // row_count)
+    row_turns = -2.0 * np.pi * index[:, None, None] * u[None] / length
+    return col_f, col_i, row_f, row_i, turns, row_turns
+
+
+def fast_device(image0, interp, vis_weight, counts, tile_index):
+    n_chan = lax.axis_size("chan")
+    n = lax.axis_size("base") * n_chan
+    row_count, length = image0.shape
+    touch = tile_index.shape[2]
+    each = touch // n
+    vcap, cells = interp.shape[3:]
+    members = cells // vcap
+    groups = touch // members
+    col_f, col_i, row_f, row_i, turns, row_turns = tables(n, row_count, length)
+    cfh, cfl = np_halves(col_f)
+    cih, cil = np_halves(col_i)
+    rfh, rfl = np_halves(row_f)
+    rih, ril = np_halves(row_i)
+    tc, ts = np.cos(turns).astype(np.float32), np.sin(turns).astype(np.float32)
+    rtc = np.cos(row_turns).astype(np.float32)
+    rts = np.sin(row_turns).astype(np.float32)
+    order = np.arange(cells).reshape(TILE_V, TILE_U).T.reshape(-1)
+    perm = np.zeros((cells, cells), np.float32)
+    perm[order, np.arange(cells)] = 1.0
+
+    live = (jnp.arange(vcap, dtype=jnp.int32)[None, :] < counts.reshape(touch, 1)).astype(F32)
+    masked = (vis_weight.reshape(touch, vcap) * live).reshape(n, 1, each * vcap)
+    masked = jnp.pad(masked, ((0, 0), (0, 0), (0, cells - each * vcap)))
+    numbers = tile_index.reshape(n, 1, each).astype(F32)
+    numbers = jnp.pad(numbers, ((0, 0), (0, 6), (0, cells - each)))
+    packed = jnp.concatenate([interp.reshape(n, each * vcap, cells), masked, numbers], axis=1)
+    packed = jnp.pad(packed, ((0, 0), (0, 72 - packed.shape[1]), (0, 0)))
+    packed = exchange(packed, n, n_chan)
+    weights = packed[:, each * vcap, : each * vcap].reshape(groups, 1, members * vcap)
+    wanted = packed[:, each * vcap + 1, :each].astype(jnp.int32).reshape(touch)
+    span = n // groups
+    wh, wl = pl.pallas_call(
+        weight_kernel,
+        grid=(groups,),
+        out_shape=[jax.ShapeDtypeStruct((groups, members * vcap, cells), BF16)] * 2,
+        in_specs=[
+            pl.BlockSpec((span, 72, cells), lambda g: (g, 0, 0)),
+            pl.BlockSpec((cells, cells), lambda g: (0, 0)),
+        ],
+        out_specs=[pl.BlockSpec((1, members * vcap, cells), lambda g: (g, 0, 0))] * 2,
+    )(packed, jnp.asarray(perm, BF16))
+
+    ready = jax.ShapeDtypeStruct((n, row_count + 8, 2 * row_count), F32)
+    wide = [pltpu.VMEM((2 * row_count, length), F32)]
+
+    def call(kernel, shapes, scratch, specs):
+        return pl.pallas_call(
+            lambda *refs: kernel(n, *refs),
+            out_shape=shapes,
+            in_specs=specs,
+            out_specs=jax.tree.map(lambda _: VMEM_SPEC, shapes),
+            scratch_shapes=scratch,
+            compiler_params=BIG,
+        )
+
+    column = call(
+        column_kernel,
+        [
+            jax.ShapeDtypeStruct((n, row_count, 2 * row_count), F32),
+            jax.ShapeDtypeStruct((8, 128), F32),
+        ],
+        [pltpu.VMEM((row_count // 16, 256, 256), F32)] * 3 + [pltpu.VMEM((2 * members, cells), F32)],
+        [SMEM_SPEC] + [VMEM_SPEC] * 10,
+    )
+    held = image0.reshape(row_count, length // n, n).transpose(1, 2, 0).reshape(length // n, -1)
+    send = call(first_kernel, ready, wide, [VMEM_SPEC] * 5)(held, rtc, rts, rfh, rfl)
+    norms = []
+    for iteration in range(ITERS):
+        arrived = exchange(send, n, n_chan)
+        back, norm = column(
+            wanted, arrived, wh, wl, weights, tc, ts, cfh, cfl, cih, cil
+        )
+        norms.append(norm[0, 0])
+        arrived = exchange(back, n, n_chan)
+        if iteration < ITERS - 1:
+            send = call(middle_kernel, ready, wide, [VMEM_SPEC] * 7)(
+                arrived, rtc, rts, rfh, rfl, rih, ril
+            )
+    held, sums = call(
+        last_kernel,
+        [
+            jax.ShapeDtypeStruct((length // n, n * row_count), F32),
+            jax.ShapeDtypeStruct((n, 8, 128), F32),
+        ],
+        wide,
+        [VMEM_SPEC] * 5,
+    )(arrived, rtc, rts, rih, ril)
+    sums = exchange(sums, n, n_chan)
+    norms.append(jnp.sqrt(jnp.sum(sums[:, 0, 0])))
+    image = held.reshape(length // n, n, row_count).transpose(2, 0, 1).reshape(row_count, length)
+    return image * (float(length) / norms[-1]), jnp.stack(norms[1:])
+
+
+def per_device(image0, interp, vis_weight, counts, tile_index):
+    n = lax.axis_size("base") * lax.axis_size("chan")
+    row_count, length = image0.shape
+    vcap, cells = interp.shape[3:]
+    touch = tile_index.shape[2]
+    fits = (n, row_count, length // row_count) == (TILE_U, 64, TILE_U)
+    if fits and (vcap, cells, touch % 256) == (8, 256, 0) and touch // n == 8:
+        return fast_device(image0, interp, vis_weight, counts, tile_index)
+    return general_device(image0, interp, vis_weight, counts, tile_index)
+
+
 def solution(mesh):
     placed = (
         P(("base", "chan"), None),

time: 1010 us -> 336 us (0.33); the launches traced: 999 us -> 336 us
  Pallas kernels: 0 us -> 319 us
  local copies, waits for them, and re-layouts: 273 us -> 7.68 us
  matrix products: 192 us -> 0 us
  blocking collectives: 172 us -> 0 us
  starting transfers between devices: 136 us -> 0 us
  waiting for transfers between devices: 126 us -> 0 us
  other arithmetic: 94.2 us -> 7.3 us
    pallas_call x0 -> x16, Pallas kernels: none -> 319 us  [the longest x8 266 us: exchange(): pl.pallas_call(lambda *refs: exchange_kernel(n, n_chan, *refs), out_shape...]
    dot_general x93 -> x0, matrix products: 192 us -> none  [the longest x12 27.9 us: transform_rows(): jnp.einsum('jp,rkp->rjk', sin_p, turned_im, precision=PRECISION_LEVEL)]
    psum x4 -> x0, blocking collectives: 162 us -> none  [total_squares(): return lax.psum(jnp.sum(image * image), ('base', 'chan'))]
    all_to_all x29 -> x0, starting transfers between devices: 136 us -> none  [the longest x6 35.7 us: transpose_global(): lax.all_to_all(real_part.reshape(1, row_count, n_base, n_chan, width), 'b...]
    all_to_all x29 -> x0, waiting for transfers between devices: 126 us -> none  [the longest x6 45.5 us: transpose_global(): lax.all_to_all(imag_part.reshape(1, row_count, n_base, n_chan, width), 'b...]
    all_to_all x27 -> x0, other arithmetic: 81.8 us -> none  [the longest x6 21.5 us: transpose_global(): lax.all_to_all(lax.all_to_all(imag_part.reshape(1, row_count, n_base, n_c...]
    unnamed x92 -> x32, local copies, waits for them, and re-layouts: 85.7 us -> 4.26 us
    mul x20 -> x1, local copies, waits for them, and re-layouts: 43.4 us -> 0.41 us  [fast_device(): return (image * (float(length) / norms[-1]), jnp.stack(norms[1:]))]
  transfers between devices with their start and end apart: 29 -> 0, of which waited for: 21 -> 0; matrix products, arithmetic and copies ran while one was open for 27% -> 0% of each run, Pallas kernels for 0% -> 0%
where the time goes in v1:
time: 336 us
  Pallas kernels  319 us (95%)
  local copies, waits for them, and re-layouts  7.68 us (2%)
  other arithmetic  7.3 us (2%)
    pallas_call x8, Pallas kernels, exchange(): pl.pallas_call(lambda *refs: exchange_kernel(n, n_chan, *refs), out_shape...  266 us
    pallas_call x3, Pallas kernels, fast_device(): column(wanted, arrived, wh, wl, weights, tc, ts, cfh, cfl, cih, cil)  38.8 us

profile of v1, /device:TPU:0, one launch (start us, length us, event | category | flops | bytes accessed | tf_op | source)
XLA Modules:
  0.0 335.7 jit_solution(5771321818906438520)
XLA Ops:
  0.6 0.8 copy.25
  1.5 0.1 reshape.92
  1.6 0.5 broadcast.60
  2.1 1.3 reduce.16
  3.4 0.1 lt.31
  3.5 0.1 copy.23
  3.6 0.1 copy.24
  3.7 0.1 lt.29
  3.8 0.7 convert_reduce_fusion.1
  4.5 0.1 convert_element_type.27
  4.6 1.8 select_maximum_fusion.refs_0_
  6.4 46.6 %shard_map.185.x_ref = f32[32,72,256]{2,1,0:T(8,128)S(1)} custom-call(f32[32,72,256]{2,1,0:T(8,128)S(1)} %select_maximum_fusion.refs_0_), custom_call_target="tpu_custom_call" | custom-call | tf_op jit(solution)/shard_map/pallas_call | solution.py:277
  53.1 0.0 copy-start
  53.1 1.4 copy-done
  54.5 0.0 copy-start.8
  54.5 6.7 %shard_map.188 = (bf16[8,256,256]{2,1,0:T(8,128)(2,1)}, bf16[8,256,256]{2,1,0:T(8,128)(2,1)}) custom-call(f32[32,72,256]{2,1,0:T(8,128)} %copy-done, bf16[256,256]{1,0:T(8,128)(2,1)} %constant.29.clone.perm_ref), custom_call_target="tpu_custom_call" | custom-call | tf_op jit(solution)/shard_map/pallas_call | solution.py:541
  61.2 0.9 slice_reduce_fusion.1
  62.1 0.1 reshape_squeeze.3.refs_4_
  62.2 1.0 convert_reduce_fusion
  63.2 0.1 convert_element_type.29.refs_0_
  63.3 0.3 copy.28
  63.6 0.4 reshape.94.refs_0_
  64.0 0.0 copy-start.5
  64.0 0.0 copy-start.6
  64.1 0.0 copy-start.11
  64.1 0.0 copy-start.12
  64.1 1.4 shard_map.186.refs_0_
  65.5 41.1 %shard_map.187.refs_1_ = f32[32,72,128]{2,1,0:T(8,128)S(1)} custom-call(f32[32,72,128]{2,1,0:T(8,128)S(1)} %shard_map.186.refs_0_), custom_call_target="tpu_custom_call" | custom-call | tf_op jit(solution)/shard_map/pallas_call | solution.py:277
  106.6 0.0 copy-start.9
  106.6 0.0 copy-start.10
  106.6 13.1 %shard_map.189 = (f32[32,64,128]{2,1,0:T(8,128)S(1)}, f32[8,128]{1,0:T(8,128)}) custom-call(s32[256]{0:T(256)S(1)} %convert_element_type.29.refs_0_, f32[32,72,128]{2,1,0:T(8,128)S(1)} %shard_map.187.refs_1_, bf16[8,256,256]{2,1,0:T(8,128)(2,1)S(1)} %copy-done.1, bf16[8,256,256]{2,1,0:T(8,128)(2,1)S(1)} %copy-done.2, ...), custom_call_target="tpu_custom_call" | custom-call | tf_op jit(solution)/shard_map/pallas_call | solution.py:579
  119.7 31.6 %shard_map.190.refs_0_ = f32[32,64,128]{2,1,0:T(8,128)S(1)} custom-call(f32[32,64,128]{2,1,0:T(8,128)S(1)} %get-tuple-element.13.refs_0_), custom_call_target="tpu_custom_call" | custom-call | tf_op jit(solution)/shard_map/pallas_call | solution.py:277
  151.4 2.5 shard_map.191.refs_0_
  153.8 31.9 %shard_map.192.refs_1_ = f32[32,72,128]{2,1,0:T(8,128)S(1)} custom-call(f32[32,72,128]{2,1,0:T(8,128)S(1)} %shard_map.191.refs_0_), custom_call_target="tpu_custom_call" | custom-call | tf_op jit(solution)/shard_map/pallas_call | solution.py:277
  185.8 12.9 %shard_map.193 = (f32[32,64,128]{2,1,0:T(8,128)S(1)}, f32[8,128]{1,0:T(8,128)S(1)}) custom-call(s32[256]{0:T(256)S(1)} %convert_element_type.29.refs_0_, f32[32,72,128]{2,1,0:T(8,128)S(1)} %shard_map.192.refs_1_, bf16[8,256,256]{2,1,0:T(8,128)(2,1)S(1)} %copy-done.1, bf16[8,256,256]{2,1,0:T(8,128)(2,1)S(1)} %copy-done.2, ...), custom_call_target="tpu_custom_call" | custom-call | tf_op jit(solution)/shard_map/pallas_call | solution.py:579
  198.7 31.6 %shard_map.194.refs_0_ = f32[32,64,128]{2,1,0:T(8,128)S(1)} custom-call(f32[32,64,128]{2,1,0:T(8,128)S(1)} %get-tuple-element.14.refs_0_), custom_call_target="tpu_custom_call" | custom-call | tf_op jit(solution)/shard_map/pallas_call | solution.py:277
  230.3 2.5 shard_map.195.refs_0_
  232.8 31.9 %shard_map.196.refs_1_ = f32[32,72,128]{2,1,0:T(8,128)S(1)} custom-call(f32[32,72,128]{2,1,0:T(8,128)S(1)} %shard_map.195.refs_0_), custom_call_target="tpu_custom_call" | custom-call | tf_op jit(solution)/shard_map/pallas_call | solution.py:277
  264.7 12.9 %shard_map.197 = (f32[32,64,128]{2,1,0:T(8,128)S(1)}, f32[8,128]{1,0:T(8,128)S(1)}) custom-call(s32[256]{0:T(256)S(1)} %convert_element_type.29.refs_0_, f32[32,72,128]{2,1,0:T(8,128)S(1)} %shard_map.196.refs_1_, bf16[8,256,256]{2,1,0:T(8,128)(2,1)S(1)} %copy-done.1, bf16[8,256,256]{2,1,0:T(8,128)(2,1)S(1)} %copy-done.2, ...), custom_call_target="tpu_custom_call" | custom-call | tf_op jit(solution)/shard_map/pallas_call | solution.py:579
  277.6 31.6 %shard_map.198.refs_0_ = f32[32,64,128]{2,1,0:T(8,128)S(1)} custom-call(f32[32,64,128]{2,1,0:T(8,128)S(1)} %get-tuple-element.15.refs_0_), custom_call_target="tpu_custom_call" | custom-call | tf_op jit(solution)/shard_map/pallas_call | solution.py:277
  309.2 1.4 shard_map.199
  310.6 19.3 %shard_map.200 = f32[32,8,128]{2,1,0:T(8,128)S(1)} custom-call(f32[32,8,128]{2,1,0:T(8,128)S(1)} %get-tuple-element.17.refs_0_), custom_call_target="tpu_custom_call" | custom-call | tf_op jit(solution)/shard_map/pallas_call | solution.py:277
  330.0 0.6 slice_reduce_fusion
  331.3 0.5 slice.19
  331.8 0.5 slice.18
  332.3 1.8 pad_maximum_fusion
  334.2 0.4 mul.21
  334.6 1.1 copy.29
  (23 shorter events, 0.1 us)
Async XLA Ops:
  53.1 1.4 copy-start
  54.5 8.8 %copy-start.13 = (f32[64,2048]{1,0:T(8,128)S(1)}, f32[64,2048]{1,0:T(8,128)}, u32[]{:S(2)}) copy-start(f32[64,2048]{1,0:T(8,128)} %param.18) | copy-start | bytes 1572868
  54.5 9.5 %copy-start.3 = (f32[32,32,128]{2,1,0:T(8,128)S(1)}, f32[32,32,128]{2,1,0:T(8,128)}, u32[]{:S(2)}) copy-start(f32[32,32,128]{2,1,0:T(8,128)} %constant.30.clone.refs_1_) | copy-start | bytes 1572868
  54.5 9.5 %copy-start.4 = (f32[32,32,128]{2,1,0:T(8,128)S(1)}, f32[32,32,128]{2,1,0:T(8,128)}, u32[]{:S(2)}) copy-start(f32[32,32,128]{2,1,0:T(8,128)} %constant.31.clone.refs_2_) | copy-start | bytes 1572868
  54.5 9.5 %copy-start.7 = (bf16[128,64]{1,0:T(8,128)(2,1)S(1)}, bf16[128,64]{1,0:T(8,128)(2,1)}, u32[]{:S(2)}) copy-start(bf16[128,64]{1,0:T(8,128)(2,1)} %constant.32.clone.refs_3_) | copy-start | bytes 49156
  54.5 9.5 %copy-start.8 = (bf16[128,64]{1,0:T(8,128)(2,1)S(1)}, bf16[128,64]{1,0:T(8,128)(2,1)}, u32[]{:S(2)}) copy-start(bf16[128,64]{1,0:T(8,128)(2,1)} %constant.33.clone.refs_4_) | copy-start | bytes 49156
  64.0 42.5 %copy-start.1 = (bf16[8,256,256]{2,1,0:T(8,128)(2,1)S(1)}, bf16[8,256,256]{2,1,0:T(8,128)(2,1)}, u32[]{:S(2)}) copy-start(bf16[8,256,256]{2,1,0:T(8,128)(2,1)} %get-tuple-element.11.refs_2_) | copy-start | bytes 3145732
  64.0 42.5 %copy-start.2 = (bf16[8,256,256]{2,1,0:T(8,128)(2,1)S(1)}, bf16[8,256,256]{2,1,0:T(8,128)(2,1)}, u32[]{:S(2)}) copy-start(bf16[8,256,256]{2,1,0:T(8,128)(2,1)} %get-tuple-element.12.refs_3_) | copy-start | bytes 3145732
  64.0 42.5 %copy-start.5 = (bf16[256,256]{1,0:T(8,128)(2,1)S(1)}, bf16[256,256]{1,0:T(8,128)(2,1)}, u32[]{:S(2)}) copy-start(bf16[256,256]{1,0:T(8,128)(2,1)} %constant.36.clone.refs_7_.refs_9_) | copy-start | bytes 393220
  64.0 42.5 %copy-start.6 = (bf16[256,256]{1,0:T(8,128)(2,1)S(1)}, bf16[256,256]{1,0:T(8,128)(2,1)}, u32[]{:S(2)}) copy-start(bf16[256,256]{1,0:T(8,128)(2,1)} %constant.37.clone.refs_8_.refs_10_) | copy-start | bytes 393220
  64.1 42.5 %copy-start.11 = (f32[32,128]{1,0:T(8,128)S(1)}, f32[32,128]{1,0:T(8,128)}, u32[]{:S(2)}) copy-start(f32[32,128]{1,0:T(8,128)} %constant.34.clone.refs_5_) | copy-start | bytes 49156
  64.1 42.5 %copy-start.12 = (f32[32,128]{1,0:T(8,128)S(1)}, f32[32,128]{1,0:T(8,128)}, u32[]{:S(2)}) copy-start(f32[32,128]{1,0:T(8,128)} %constant.35.clone.refs_6_) | copy-start | bytes 49156
  106.6 44.7 %copy-start.9 = (bf16[64,128]{1,0:T(8,128)(2,1)S(1)}, bf16[64,128]{1,0:T(8,128)(2,1)}, u32[]{:S(2)}) copy-start(bf16[64,128]{1,0:T(8,128)(2,1)} %constant.38.clone.refs_5_.refs_3_) | copy-start | bytes 49156
  106.6 44.7 %copy-start.10 = (bf16[64,128]{1,0:T(8,128)(2,1)S(1)}, bf16[64,128]{1,0:T(8,128)(2,1)}, u32[]{:S(2)}) copy-start(bf16[64,128]{1,0:T(8,128)(2,1)} %constant.39.clone.refs_6_.refs_4_) | copy-start | bytes 49156

commit v2 on v1

--- a/solution.py
+++ b/solution.py
@@ -244,50 +244,66 @@
     return low + high
 
 
-def exchange_kernel(n, n_chan, src_ref, dst_ref, own_sem, send_sem, recv_sem):
+def exchange_kernel(n, n_chan, count, *refs):
+    sources, targets = refs[:count], refs[count : 2 * count]
+    own_sem, send_sem, recv_sem = refs[2 * count :]
     me = lax.axis_index("base") * n_chan + lax.axis_index("chan")
-    own = pltpu.make_async_copy(src_ref.at[me], dst_ref.at[me], own_sem)
-    own.start()
-
-    def copy(step):
+
+    def copies(step):
         peer = lax.rem(me + step, n)
-        return pltpu.make_async_remote_copy(
-            src_ref=src_ref.at[peer],
-            dst_ref=dst_ref.at[me],
-            send_sem=send_sem.at[step],
-            recv_sem=recv_sem.at[step],
-            device_id=(peer // n_chan, lax.rem(peer, n_chan)),
-            device_id_type=pl.DeviceIdType.MESH,
-        )
+        return [
+            pltpu.make_async_remote_copy(
+                src_ref=sources[k].at[peer],
+                dst_ref=targets[k].at[me],
+                send_sem=send_sem.at[k, step],
+                recv_sem=recv_sem.at[k, step],
+                device_id=(peer // n_chan, lax.rem(peer, n_chan)),
+                device_id_type=pl.DeviceIdType.MESH,
+            )
+            for k in range(count)
+        ]
 
     def launch(step, carry):
-        copy(step).start()
+        for copy in copies(step):
+            copy.start()
         return carry
 
     def finish(step, carry):
-        copy(step).wait()
+        for copy in copies(step):
+            copy.wait()
         return carry
 
+    own = [
+        pltpu.make_async_copy(sources[k].at[me], targets[k].at[me], own_sem.at[k])
+        for k in range(count)
+    ]
     lax.fori_loop(1, n, launch, 0)
-    own.wait()
+    for copy in own:
+        copy.start()
+    for copy in own:
+        copy.wait()
     lax.fori_loop(1, n, finish, 0)
 
 
-def exchange(values, n, n_chan):
+def exchange(arrays, n, n_chan):
+    count = len(arrays)
     return pl.pallas_call(
-        lambda *refs: exchange_kernel(n, n_chan, *refs),
-        out_shape=jax.ShapeDtypeStruct(values.shape, values.dtype),
-        in_specs=[pl.BlockSpec(memory_space=pltpu.VMEM)],
-        out_specs=pl.BlockSpec(memory_space=pltpu.VMEM),
+        lambda *refs: exchange_kernel(n, n_chan, count, *refs),
+        out_shape=[jax.ShapeDtypeStruct(values.shape, values.dtype) for values in arrays],
+        in_specs=[
+            pl.BlockSpec(memory_space=pl.ANY) if values.size * 4 > 2**20 else VMEM_SPEC
+            for values in arrays
+        ],
+        out_specs=[VMEM_SPEC] * count,
         scratch_shapes=[
-            pltpu.SemaphoreType.DMA,
-            pltpu.SemaphoreType.DMA((n,)),
-            pltpu.SemaphoreType.DMA((n,)),
+            pltpu.SemaphoreType.DMA((count,)),
+            pltpu.SemaphoreType.DMA((count, n)),
+            pltpu.SemaphoreType.DMA((count, n)),
         ],
         compiler_params=pltpu.CompilerParams(
             has_side_effects=True, vmem_limit_bytes=48 * 1024 * 1024
         ),
-    )(values)
+    )(*arrays)
 
 
 def turn(re, im, c, s):
@@ -332,7 +348,7 @@
     return parts
 
 
-def row_forward(n, parts, tc_ref, ts_ref, mh_ref, ml_ref, b_ref, send_ref):
+def row_forward(n, parts, tc_ref, ts_ref, mh_ref, ml_ref, b_ref, send_ref, sum_ref):
     rows = tc_ref.shape[1]
     total = sum(jnp.sum(part * part) for part in parts)
     for index, part in enumerate(parts):
@@ -361,17 +377,17 @@
 
     lax.fori_loop(0, rows // 8, chunk, 0)
     for o in range(n):
-        send_ref[o, 2 * rows : 2 * rows + 8, :] = jnp.full((8, 128), total, F32)
-
-
-def first_kernel(n, y_ref, tc, ts, fh, fl, send_ref, b_ref):
+        sum_ref[o] = jnp.full((1, 128), total, F32)
+
+
+def first_kernel(n, y_ref, tc, ts, fh, fl, send_ref, sum_ref, b_ref):
     parts = [y_ref[:, s : s + 512] for s in range(0, y_ref.shape[1], 512)]
-    row_forward(n, parts, tc, ts, fh, fl, b_ref, send_ref)
-
-
-def middle_kernel(n, recv_ref, tc, ts, fh, fl, ih, il, send_ref, b_ref):
+    row_forward(n, parts, tc, ts, fh, fl, b_ref, send_ref, sum_ref)
+
+
+def middle_kernel(n, recv_ref, tc, ts, fh, fl, ih, il, send_ref, sum_ref, b_ref):
     parts = row_inverse(n, recv_ref, tc, ts, ih, il, b_ref)
-    row_forward(n, parts, tc, ts, fh, fl, b_ref, send_ref)
+    row_forward(n, parts, tc, ts, fh, fl, b_ref, send_ref, sum_ref)
 
 
 def last_kernel(n, recv_ref, tc, ts, ih, il, y_ref, sum_ref, b_ref):
@@ -380,13 +396,14 @@
         y_ref[:, index * 512 : (index + 1) * 512] = part
     total = sum(jnp.sum(part * part) for part in parts)
     for o in range(n):
-        sum_ref[o] = jnp.full((8, 128), total, F32)
+        sum_ref[o] = jnp.full((1, 128), total, F32)
 
 
 def column_kernel(
     n,
     tile_ref,
     recv_ref,
+    sum_ref,
     wh_ref,
     wl_ref,
     wm_ref,
@@ -407,10 +424,9 @@
     blocks = rows // 8
     groups = wh_ref.shape[0]
     members = g_ref.shape[0] // 2
-    across = 2 * rows
-    total = recv_ref[0, 2 * rows : 2 * rows + 8, :]
+    total = sum_ref[0]
     for d in range(1, n):
-        total = total + recv_ref[d, 2 * rows : 2 * rows + 8, :]
+        total = total + sum_ref[d]
     norm = jnp.sqrt(total)
     norm_ref[...] = norm
 
@@ -432,8 +448,9 @@
             u_ref[i, k * 8 : k * 8 + 8, :128] = re
             u_ref[i, k * 8 : k * 8 + 8, 128:] = im
         right = halves(u_ref[i])
-        t_ref[i] = triple_dot((fh[...], fl[...]), right, ((1,), (1,)))
-        acc_ref[i] = jnp.zeros(acc_ref.shape[1:], F32)
+        at = pl.ds(pl.multiple_of(i * 256, 256), 256)
+        t_ref[at, :] = triple_dot((fh[...], fl[...]), right, ((1,), (1,)))
+        acc_ref[at, :] = jnp.zeros((256, acc_ref.shape[1]), F32)
         return carry
 
     lax.fori_loop(0, blocks, forward, 0)
@@ -441,32 +458,27 @@
     row_of = lax.broadcasted_iota(jnp.int32, (2 * members, 256), 0) % members
     slot_of = lax.broadcasted_iota(jnp.int32, (2 * members, 256), 1) // (256 // members)
 
-    def place(index):
-        tile = tile_ref[index]
-        column = tile // across
-        row = (column // blocks) * across + tile % across
-        return column % blocks, row
-
     def group(g, carry):
         for s in range(members):
-            block, row = place(g * members + s)
-            g_ref[s : s + 1, :] = t_ref[block, pl.ds(row, 1), :]
-            g_ref[s + members : s + members + 1, :] = t_ref[block, pl.ds(row + 128, 1), :]
+            row = tile_ref[g * members + s]
+            g_ref[s : s + 1, :] = t_ref[pl.ds(row, 1), :]
+            g_ref[s + members : s + members + 1, :] = t_ref[pl.ds(row + 128, 1), :]
         weights = (wh_ref[g], wl_ref[g])
         seen = triple_dot(halves(g_ref[...]), weights, ((1,), (1,)))
         seen = jnp.where(row_of == slot_of, seen * wm_ref[g], 0.0)
         g_ref[...] = triple_dot(halves(seen), weights, ((1,), (0,)))
         for s in range(members):
-            block, row = place(g * members + s)
-            acc_ref[block, pl.ds(row, 1), :] += g_ref[s : s + 1, :]
-            acc_ref[block, pl.ds(row + 128, 1), :] += g_ref[s + members : s + members + 1, :]
+            row = tile_ref[g * members + s]
+            acc_ref[pl.ds(row, 1), :] += g_ref[s : s + 1, :]
+            acc_ref[pl.ds(row + 128, 1), :] += g_ref[s + members : s + members + 1, :]
         return carry
 
     lax.fori_loop(0, groups, group, 0)
 
     def backward(i, carry):
         at = pl.multiple_of(i * 8, 8)
-        u_ref[i] = triple_dot(halves(acc_ref[i].T), (ih[...], il[...]), ((1,), (0,)))
+        held = acc_ref[pl.ds(pl.multiple_of(i * 256, 256), 256), :]
+        u_ref[i] = triple_dot(halves(held.T), (ih[...], il[...]), ((1,), (0,)))
         items = []
         for k in range(n):
             re = u_ref[i, k * 8 : k * 8 + 8, :128]
@@ -483,7 +495,7 @@
 
 def weight_kernel(x_ref, perm_ref, high_ref, low_ref):
     count, _, cells = x_ref.shape
-    value = x_ref[:, :64, :].reshape(count * 64, cells)
+    value = x_ref[...].reshape(count * x_ref.shape[1], cells)
     for part, ref in zip(halves(value), (high_ref, low_ref)):
         ref[0] = jnp.dot(part, perm_ref[...], preferred_element_type=F32).astype(BF16)
 
@@ -529,28 +541,14 @@
 
     live = (jnp.arange(vcap, dtype=jnp.int32)[None, :] < counts.reshape(touch, 1)).astype(F32)
     masked = (vis_weight.reshape(touch, vcap) * live).reshape(n, 1, each * vcap)
-    masked = jnp.pad(masked, ((0, 0), (0, 0), (0, cells - each * vcap)))
     numbers = tile_index.reshape(n, 1, each).astype(F32)
-    numbers = jnp.pad(numbers, ((0, 0), (0, 6), (0, cells - each)))
-    packed = jnp.concatenate([interp.reshape(n, each * vcap, cells), masked, numbers], axis=1)
-    packed = jnp.pad(packed, ((0, 0), (0, 72 - packed.shape[1]), (0, 0)))
-    packed = exchange(packed, n, n_chan)
-    weights = packed[:, each * vcap, : each * vcap].reshape(groups, 1, members * vcap)
-    wanted = packed[:, each * vcap + 1, :each].astype(jnp.int32).reshape(touch)
-    span = n // groups
-    wh, wl = pl.pallas_call(
-        weight_kernel,
-        grid=(groups,),
-        out_shape=[jax.ShapeDtypeStruct((groups, members * vcap, cells), BF16)] * 2,
-        in_specs=[
-            pl.BlockSpec((span, 72, cells), lambda g: (g, 0, 0)),
-            pl.BlockSpec((cells, cells), lambda g: (0, 0)),
-        ],
-        out_specs=[pl.BlockSpec((1, members * vcap, cells), lambda g: (g, 0, 0))] * 2,
-    )(packed, jnp.asarray(perm, BF16))
-
-    ready = jax.ShapeDtypeStruct((n, row_count + 8, 2 * row_count), F32)
+    extras = jnp.concatenate([masked, numbers], axis=2)
+    extras = jnp.pad(extras, ((0, 0), (0, 0), (0, -extras.shape[2] % 128)))
+    matrices = interp.reshape(n, each * vcap, cells)
     wide = [pltpu.VMEM((2 * row_count, length), F32)]
+    data = jax.ShapeDtypeStruct((n, row_count, 2 * row_count), F32)
+    mark = jax.ShapeDtypeStruct((n, 1, 128), F32)
+    ready = [data, mark]
 
     def call(kernel, shapes, scratch, specs):
         return pl.pallas_call(
@@ -562,39 +560,60 @@
             compiler_params=BIG,
         )
 
+    held = image0.reshape(row_count, length // n, n).transpose(1, 2, 0).reshape(length // n, -1)
+    send = call(first_kernel, ready, wide, [VMEM_SPEC] * 5)(held, rtc, rts, rfh, rfl)
+    arrived, sums, extras, matrices = exchange([*send, extras, matrices], n, n_chan)
+    weights = extras[:, 0, : each * vcap].reshape(groups, 1, members * vcap)
+    wanted = extras[:, 0, each * vcap : each * (vcap + 1)].astype(jnp.int32).reshape(touch)
+    down = length // TILE_U
+    blocks = row_count // TILE_V // 2
+    tile_column = wanted // down
+    wanted = (tile_column % blocks) * (4 * down) + (tile_column // blocks) * down + wanted % down
+    span = n // groups
+    wh, wl = pl.pallas_call(
+        weight_kernel,
+        grid=(groups,),
+        out_shape=[jax.ShapeDtypeStruct((groups, members * vcap, cells), BF16)] * 2,
+        in_specs=[
+            pl.BlockSpec((span, each * vcap, cells), lambda g: (g, 0, 0)),
+            pl.BlockSpec((cells, cells), lambda g: (0, 0)),
+        ],
+        out_specs=[pl.BlockSpec((1, members * vcap, cells), lambda g: (g, 0, 0))] * 2,
+    )(matrices, jnp.asarray(perm, BF16))
+
     column = call(
         column_kernel,
         [
-            jax.ShapeDtypeStruct((n, row_count, 2 * row_count), F32),
-            jax.ShapeDtypeStruct((8, 128), F32),
+            data,
+            jax.ShapeDtypeStruct((1, 128), F32),
         ],
-        [pltpu.VMEM((row_count // 16, 256, 256), F32)] * 3 + [pltpu.VMEM((2 * members, cells), F32)],
-        [SMEM_SPEC] + [VMEM_SPEC] * 10,
-    )
-    held = image0.reshape(row_count, length // n, n).transpose(1, 2, 0).reshape(length // n, -1)
-    send = call(first_kernel, ready, wide, [VMEM_SPEC] * 5)(held, rtc, rts, rfh, rfl)
+        [pltpu.VMEM((blocks, 256, 256), F32)]
+        + [pltpu.VMEM((blocks * 256, 256), F32)] * 2
+        + [pltpu.VMEM((2 * members, cells), F32)],
+        [SMEM_SPEC] + [VMEM_SPEC] * 11,
+    )
     norms = []
     for iteration in range(ITERS):
-        arrived = exchange(send, n, n_chan)
-        back, norm = column(
-            wanted, arrived, wh, wl, weights, tc, ts, cfh, cfl, cih, cil
-        )
-        norms.append(norm[0, 0])
-        arrived = exchange(back, n, n_chan)
-        if iteration < ITERS - 1:
+        if iteration > 0:
             send = call(middle_kernel, ready, wide, [VMEM_SPEC] * 7)(
                 arrived, rtc, rts, rfh, rfl, rih, ril
             )
+            arrived, sums = exchange(send, n, n_chan)
+        back, norm = column(
+            wanted, arrived, sums, wh, wl, weights, tc, ts, cfh, cfl, cih, cil
+        )
+        norms.append(norm[0, 0])
+        (arrived,) = exchange([back], n, n_chan)
     held, sums = call(
         last_kernel,
         [
             jax.ShapeDtypeStruct((length // n, n * row_count), F32),
-            jax.ShapeDtypeStruct((n, 8, 128), F32),
+            mark,
         ],
         wide,
         [VMEM_SPEC] * 5,
     )(arrived, rtc, rts, rih, ril)
-    sums = exchange(sums, n, n_chan)
+    (sums,) = exchange([sums], n, n_chan)
     norms.append(jnp.sqrt(jnp.sum(sums[:, 0, 0])))
     image = held.reshape(length // n, n, row_count).transpose(2, 0, 1).reshape(row_count, length)
     return image * (float(length) / norms[-1]), jnp.stack(norms[1:])

time: 336 us -> 307 us (0.914)
  Pallas kernels: 319 us -> 292 us
  other arithmetic: 7.3 us -> 3.6 us
    pallas_call x11 -> x10, Pallas kernels: 305 us -> 278 us  [the longest x7 249 us: exchange(): pl.pallas_call(lambda *refs: exchange_kernel(n, n_chan, count, *refs), ou...]
    unnamed x32 -> x34, local copies, waits for them, and re-layouts: 4.26 us -> 7.68 us
where the time goes in v2:
time: 307 us; the launch traced here: 306 us
  Pallas kernels  292 us (95%)
  local copies, waits for them, and re-layouts  9.16 us (3%)
  other arithmetic  3.6 us (1%)
    pallas_call x7, Pallas kernels, exchange(): pl.pallas_call(lambda *refs: exchange_kernel(n, n_chan, count, *refs), ou...  249 us
    pallas_call x3, Pallas kernels, fast_device(): column(wanted, arrived, sums, wh, wl, weights, tc, ts, cfh, cfl, cih, cil)  28.4 us
    unnamed x34, local copies, waits for them, and re-layouts  7.68 us
    pallas_call x1, Pallas kernels, fast_device(): pl.pallas_call(weight_kernel, grid=(groups,), out_shape=[jax.ShapeDtypeSt...  6.46 us

profile of v2, /device:TPU:0, one launch (start us, length us, event | category | flops | bytes accessed | tf_op | source)
XLA Modules:
  0.0 306.3 jit_solution(172716760038256132)
XLA Ops:
  0.6 0.0 copy-start.4
  0.6 0.0 copy-start.5
  0.7 0.0 copy-start.9
  0.7 0.0 copy-start.10
  0.7 0.5 broadcast.77
  1.2 1.3 reduce.16
  2.5 0.7 convert_reduce_fusion.1
  3.2 0.1 lt.39
  3.3 0.1 convert_element_type.25
  3.4 0.1 lt.41
  3.5 0.1 copy.24
  3.6 0.1 copy.25
  3.6 0.8 copy.26
  4.5 0.1 reshape.93
  4.6 0.1 fusion.refs_2_
  4.7 1.4 copy.23
  6.1 0.4 reshape.92.refs_0_
  6.5 1.4 shard_map.185
  7.9 0.0 copy-start.6
  8.0 0.0 copy-start.7
  8.0 0.0 copy-start.13
  8.0 0.0 copy-start.14
  8.0 61.6 %shard_map.186 = (f32[32,64,128]{2,1,0:T(8,128)S(1)}, f32[32,1,128]{2,1,0:T(1,128)S(1)}, f32[32,1,128]{2,1,0:T(1,128)S(1)}, f32[32,64,256]{2,1,0:T(8,128)S(1)}) custom-call(f32[32,64,128]{2,1,0:T(8,128)S(1)} %get-tuple-element.25.refs_0_, f32[32,1,128]{2,1,0:T(1,128)S(1)} %get-tuple-element.26.refs_1_, f32[32,1,128]{2,1,0:T(1,128)S(1)} %fusion.refs_2_, ...), custom_call_target="tpu_custom_call" | custom-call | tf_op jit(solution)/shard_map/pallas_call | solution.py:290
  69.6 1.3 copy-done.8
  71.0 0.1 reshape_squeeze.3.refs_5_
  71.1 0.1 convert_reduce_fusion
  71.2 0.1 convert_element_type.27
  71.3 6.5 %shard_map.187 = (bf16[8,256,256]{2,1,0:T(8,128)(2,1)}, bf16[8,256,256]{2,1,0:T(8,128)(2,1)}) custom-call(f32[32,64,256]{2,1,0:T(8,128)} %copy-done.8, bf16[256,256]{1,0:T(8,128)(2,1)} %constant.84.clone.perm_ref), custom_call_target="tpu_custom_call" | custom-call | tf_op jit(solution)/shard_map/pallas_call | solution.py:573
  77.8 0.0 copy-done.13
  77.8 0.0 copy-done.14
  77.8 1.2 copy-done
  79.0 1.2 copy-done.2
  80.3 9.5 %shard_map.188 = (f32[32,64,128]{2,1,0:T(8,128)S(1)}, f32[1,128]{1,0:T(1,128)}) custom-call(s32[256]{0:T(256)S(1)} %fusion.3.refs_0_, f32[32,64,128]{2,1,0:T(8,128)S(1)} %get-tuple-element.28.refs_1_, f32[32,1,128]{2,1,0:T(1,128)S(1)} %get-tuple-element.29.refs_2_, bf16[8,256,256]{2,1,0:T(8,128)(2,1)S(1)} %copy-done, bf16[8,256,256]{2,1,0:T(8,128)(2,1)S(1)} %copy-done.2, ...), custom_call_target="tpu_custom_call" | custom-call | tf_op jit(solution)/shard_map/pallas_call | solution.py:602
  89.8 45.1 %shard_map.189.refs_0_ = f32[32,64,128]{2,1,0:T(8,128)S(1)} custom-call(f32[32,64,128]{2,1,0:T(8,128)S(1)} %get-tuple-element.33.refs_0_), custom_call_target="tpu_custom_call" | custom-call | tf_op jit(solution)/shard_map/pallas_call | solution.py:290
  134.9 2.5 shard_map.190
  137.5 31.0 %shard_map.191 = (f32[32,64,128]{2,1,0:T(8,128)S(1)}, f32[32,1,128]{2,1,0:T(1,128)S(1)}) custom-call(f32[32,64,128]{2,1,0:T(8,128)S(1)} %get-tuple-element.34.refs_0_, f32[32,1,128]{2,1,0:T(1,128)S(1)} %get-tuple-element.35.refs_1_), custom_call_target="tpu_custom_call" | custom-call | tf_op jit(solution)/shard_map/pallas_call | solution.py:290
  168.5 9.4 %shard_map.192 = (f32[32,64,128]{2,1,0:T(8,128)S(1)}, f32[1,128]{1,0:T(1,128)S(1)}) custom-call(s32[256]{0:T(256)S(1)} %fusion.3.refs_0_, f32[32,64,128]{2,1,0:T(8,128)S(1)} %get-tuple-element.36.refs_1_, f32[32,1,128]{2,1,0:T(1,128)S(1)} %get-tuple-element.37.refs_2_, bf16[8,256,256]{2,1,0:T(8,128)(2,1)S(1)} %copy-done.1, ...), custom_call_target="tpu_custom_call" | custom-call | tf_op jit(solution)/shard_map/pallas_call | solution.py:602
  177.9 30.7 %shard_map.193.refs_0_ = f32[32,64,128]{2,1,0:T(8,128)S(1)} custom-call(f32[32,64,128]{2,1,0:T(8,128)S(1)} %get-tuple-element.38.refs_0_), custom_call_target="tpu_custom_call" | custom-call | tf_op jit(solution)/shard_map/pallas_call | solution.py:290
  208.6 2.5 shard_map.194
  211.1 31.0 %shard_map.195 = (f32[32,64,128]{2,1,0:T(8,128)S(1)}, f32[32,1,128]{2,1,0:T(1,128)S(1)}) custom-call(f32[32,64,128]{2,1,0:T(8,128)S(1)} %get-tuple-element.39.refs_0_, f32[32,1,128]{2,1,0:T(1,128)S(1)} %get-tuple-element.40.refs_1_), custom_call_target="tpu_custom_call" | custom-call | tf_op jit(solution)/shard_map/pallas_call | solution.py:290
  242.1 9.4 %shard_map.196 = (f32[32,64,128]{2,1,0:T(8,128)S(1)}, f32[1,128]{1,0:T(1,128)S(1)}) custom-call(s32[256]{0:T(256)S(1)} %fusion.3.refs_0_, f32[32,64,128]{2,1,0:T(8,128)S(1)} %get-tuple-element.41.refs_1_, f32[32,1,128]{2,1,0:T(1,128)S(1)} %get-tuple-element.42.refs_2_, bf16[8,256,256]{2,1,0:T(8,128)(2,1)S(1)} %copy-done.1, ...), custom_call_target="tpu_custom_call" | custom-call | tf_op jit(solution)/shard_map/pallas_call | solution.py:602
  251.6 30.7 %shard_map.197.refs_0_ = f32[32,64,128]{2,1,0:T(8,128)S(1)} custom-call(f32[32,64,128]{2,1,0:T(8,128)S(1)} %get-tuple-element.43.refs_0_), custom_call_target="tpu_custom_call" | custom-call | tf_op jit(solution)/shard_map/pallas_call | solution.py:290
  282.2 1.4 shard_map.198
  283.6 19.1 %shard_map.199 = f32[32,1,128]{2,1,0:T(1,128)S(1)} custom-call(f32[32,1,128]{2,1,0:T(1,128)S(1)} %get-tuple-element.45.refs_0_), custom_call_target="tpu_custom_call" | custom-call | tf_op jit(solution)/shard_map/pallas_call | solution.py:290
  302.7 0.6 slice_reduce_fusion
  304.1 0.6 pad_maximum_fusion
  304.8 0.4 mul.34
  305.2 1.1 copy.29
  (23 shorter events, 0.2 us)
Async XLA Ops:
  0.6 5.8 %copy-start.4 = (f32[32,32,128]{2,1,0:T(8,128)S(1)}, f32[32,32,128]{2,1,0:T(8,128)}, u32[]{:S(2)}) copy-start(f32[32,32,128]{2,1,0:T(8,128)} %constant.81.clone.refs_2_) | copy-start | bytes 1572868
  0.6 5.8 %copy-start.5 = (f32[32,32,128]{2,1,0:T(8,128)S(1)}, f32[32,32,128]{2,1,0:T(8,128)}, u32[]{:S(2)}) copy-start(f32[32,32,128]{2,1,0:T(8,128)} %constant.80.clone.refs_1_) | copy-start | bytes 1572868
  0.7 5.8 %copy-start.9 = (bf16[128,64]{1,0:T(8,128)(2,1)S(1)}, bf16[128,64]{1,0:T(8,128)(2,1)}, u32[]{:S(2)}) copy-start(bf16[128,64]{1,0:T(8,128)(2,1)} %constant.83.clone.refs_4_) | copy-start | bytes 49156
  0.7 5.8 %copy-start.10 = (bf16[128,64]{1,0:T(8,128)(2,1)S(1)}, bf16[128,64]{1,0:T(8,128)(2,1)}, u32[]{:S(2)}) copy-start(bf16[128,64]{1,0:T(8,128)(2,1)} %constant.82.clone.refs_3_) | copy-start | bytes 49156
  7.9 69.8 %copy-start.6 = (bf16[256,256]{1,0:T(8,128)(2,1)S(1)}, bf16[256,256]{1,0:T(8,128)(2,1)}, u32[]{:S(2)}) copy-start(bf16[256,256]{1,0:T(8,128)(2,1)} %constant.88.clone.refs_9_.refs_11_) | copy-start | bytes 393220
  8.0 69.8 %copy-start.7 = (bf16[256,256]{1,0:T(8,128)(2,1)S(1)}, bf16[256,256]{1,0:T(8,128)(2,1)}, u32[]{:S(2)}) copy-start(bf16[256,256]{1,0:T(8,128)(2,1)} %constant.87.clone.refs_8_.refs_10_) | copy-start | bytes 393220
  8.0 69.8 %copy-start.13 = (f32[32,128]{1,0:T(8,128)S(1)}, f32[32,128]{1,0:T(8,128)}, u32[]{:S(2)}) copy-start(f32[32,128]{1,0:T(8,128)} %constant.86.clone.refs_7_) | copy-start | bytes 49156
  8.0 69.8 %copy-start.14 = (f32[32,128]{1,0:T(8,128)S(1)}, f32[32,128]{1,0:T(8,128)}, u32[]{:S(2)}) copy-start(f32[32,128]{1,0:T(8,128)} %constant.85.clone.refs_6_) | copy-start | bytes 49156
  69.6 1.3 copy-start.8
  77.8 1.2 copy-start
  79.0 1.2 copy-start.2
  80.3 54.6 %copy-start.11 = (bf16[64,128]{1,0:T(8,128)(2,1)S(1)}, bf16[64,128]{1,0:T(8,128)(2,1)}, u32[]{:S(2)}) copy-start(bf16[64,128]{1,0:T(8,128)(2,1)} %constant.90.clone.refs_6_.refs_4_) | copy-start | bytes 49156
  80.3 54.6 %copy-start.12 = (bf16[64,128]{1,0:T(8,128)(2,1)S(1)}, bf16[64,128]{1,0:T(8,128)(2,1)}, u32[]{:S(2)}) copy-start(bf16[64,128]{1,0:T(8,128)(2,1)} %constant.89.clone.refs_5_.refs_3_) | copy-start | bytes 49156
  134.9 33.6 %copy-start.1 = (bf16[8,256,256]{2,1,0:T(8,128)(2,1)S(1)}, bf16[8,256,256]{2,1,0:T(8,128)(2,1)}, u32[]{:S(2)}) copy-start(bf16[8,256,256]{2,1,0:T(8,128)(2,1)} %get-tuple-element.31.refs_3_) | copy-start | bytes 3145732
  134.9 33.6 %copy-start.3 = (bf16[8,256,256]{2,1,0:T(8,128)(2,1)S(1)}, bf16[8,256,256]{2,1,0:T(8,128)(2,1)}, u32[]{:S(2)}) copy-start(bf16[8,256,256]{2,1,0:T(8,128)(2,1)} %get-tuple-element.32.refs_4_) | copy-start | bytes 3145732

commit v3 on v2

--- a/solution.py
+++ b/solution.py
@@ -497,7 +497,11 @@
     count, _, cells = x_ref.shape
     value = x_ref[...].reshape(count * x_ref.shape[1], cells)
     for part, ref in zip(halves(value), (high_ref, low_ref)):
-        ref[0] = jnp.dot(part, perm_ref[...], preferred_element_type=F32).astype(BF16)
+        ref[...] = (
+            jnp.dot(part, perm_ref[...], preferred_element_type=F32)
+            .astype(BF16)
+            .reshape(ref.shape)
+        )
 
 
 def tables(n, row_count, length):
@@ -569,16 +573,17 @@
     blocks = row_count // TILE_V // 2
     tile_column = wanted // down
     wanted = (tile_column % blocks) * (4 * down) + (tile_column // blocks) * down + wanted % down
-    span = n // groups
+    joint = math.gcd(groups, 4)
+    span = n // groups * joint
     wh, wl = pl.pallas_call(
         weight_kernel,
-        grid=(groups,),
+        grid=(groups // joint,),
         out_shape=[jax.ShapeDtypeStruct((groups, members * vcap, cells), BF16)] * 2,
         in_specs=[
             pl.BlockSpec((span, each * vcap, cells), lambda g: (g, 0, 0)),
             pl.BlockSpec((cells, cells), lambda g: (0, 0)),
         ],
-        out_specs=[pl.BlockSpec((1, members * vcap, cells), lambda g: (g, 0, 0))] * 2,
+        out_specs=[pl.BlockSpec((joint, members * vcap, cells), lambda g: (g, 0, 0))] * 2,
     )(matrices, jnp.asarray(perm, BF16))
 
     column = call(

time: 307 us -> 303 us (0.987)
  Pallas kernels: 292 us -> 288 us
    pallas_call x1, Pallas kernels: 6.46 us -> 3.15 us  [fast_device(): pl.pallas_call(weight_kernel, grid=(groups // joint,), out_shape=[jax.Sha...]
where the time goes in v3:
time: 303 us
  Pallas kernels  288 us (95%)
  local copies, waits for them, and re-layouts  9.16 us (3%)
  other arithmetic  3.6 us (1%)
    pallas_call x7, Pallas kernels, exchange(): pl.pallas_call(lambda *refs: exchange_kernel(n, n_chan, count, *refs), ou...  249 us
    pallas_call x3, Pallas kernels, fast_device(): column(wanted, arrived, sums, wh, wl, weights, tc, ts, cfh, cfl, cih, cil)  28.3 us
    unnamed x34, local copies, waits for them, and re-layouts  7.68 us

profile of v3, /device:TPU:0, one launch (start us, length us, event | category | flops | bytes accessed | tf_op | source)
XLA Modules:
  0.0 303.0 jit_solution(9656166899448852497)
XLA Ops:
  0.6 0.0 copy-start.4
  0.6 0.0 copy-start.5
  0.7 0.0 copy-start.9
  0.7 0.0 copy-start.10
  0.7 0.5 broadcast.77
  1.2 1.3 reduce.16
  2.5 0.7 convert_reduce_fusion.1
  3.2 0.1 lt.39
  3.3 0.1 convert_element_type.25
  3.4 0.1 lt.41
  3.5 0.1 copy.24
  3.6 0.1 copy.25
  3.6 0.8 copy.26
  4.5 0.1 reshape.93
  4.6 0.1 fusion.refs_2_
  4.7 1.4 copy.23
  6.1 0.4 reshape.92.refs_0_
  6.5 1.4 shard_map.185
  7.9 0.0 copy-start.6
  8.0 0.0 copy-start.7
  8.0 0.0 copy-start.13
  8.0 0.0 copy-start.14
  8.0 61.6 %shard_map.186 = (f32[32,64,128]{2,1,0:T(8,128)S(1)}, f32[32,1,128]{2,1,0:T(1,128)S(1)}, f32[32,1,128]{2,1,0:T(1,128)S(1)}, f32[32,64,256]{2,1,0:T(8,128)S(1)}) custom-call(f32[32,64,128]{2,1,0:T(8,128)S(1)} %get-tuple-element.25.refs_0_, f32[32,1,128]{2,1,0:T(1,128)S(1)} %get-tuple-element.26.refs_1_, f32[32,1,128]{2,1,0:T(1,128)S(1)} %fusion.refs_2_, ...), custom_call_target="tpu_custom_call" | custom-call | tf_op jit(solution)/shard_map/pallas_call | solution.py:290
  69.6 1.3 copy-done.8
  71.0 0.1 reshape_squeeze.3.refs_5_
  71.1 0.1 convert_reduce_fusion
  71.2 0.1 convert_element_type.27
  71.3 3.2 %shard_map.187 = (bf16[8,256,256]{2,1,0:T(8,128)(2,1)}, bf16[8,256,256]{2,1,0:T(8,128)(2,1)}) custom-call(f32[32,64,256]{2,1,0:T(8,128)} %copy-done.8, bf16[256,256]{1,0:T(8,128)(2,1)} %constant.84.clone.perm_ref), custom_call_target="tpu_custom_call" | custom-call | tf_op jit(solution)/shard_map/pallas_call | solution.py:578
  74.5 0.0 copy-done.13
  74.5 0.0 copy-done.14
  74.5 1.2 copy-done
  75.7 1.2 copy-done.2
  77.0 9.5 %shard_map.188 = (f32[32,64,128]{2,1,0:T(8,128)S(1)}, f32[1,128]{1,0:T(1,128)}) custom-call(s32[256]{0:T(256)S(1)} %fusion.3.refs_0_, f32[32,64,128]{2,1,0:T(8,128)S(1)} %get-tuple-element.28.refs_1_, f32[32,1,128]{2,1,0:T(1,128)S(1)} %get-tuple-element.29.refs_2_, bf16[8,256,256]{2,1,0:T(8,128)(2,1)S(1)} %copy-done, bf16[8,256,256]{2,1,0:T(8,128)(2,1)S(1)} %copy-done.2, ...), custom_call_target="tpu_custom_call" | custom-call | tf_op jit(solution)/shard_map/pallas_call | solution.py:607
  86.5 45.1 %shard_map.189.refs_0_ = f32[32,64,128]{2,1,0:T(8,128)S(1)} custom-call(f32[32,64,128]{2,1,0:T(8,128)S(1)} %get-tuple-element.33.refs_0_), custom_call_target="tpu_custom_call" | custom-call | tf_op jit(solution)/shard_map/pallas_call | solution.py:290
  131.6 2.5 shard_map.190
  134.2 31.0 %shard_map.191 = (f32[32,64,128]{2,1,0:T(8,128)S(1)}, f32[32,1,128]{2,1,0:T(1,128)S(1)}) custom-call(f32[32,64,128]{2,1,0:T(8,128)S(1)} %get-tuple-element.34.refs_0_, f32[32,1,128]{2,1,0:T(1,128)S(1)} %get-tuple-element.35.refs_1_), custom_call_target="tpu_custom_call" | custom-call | tf_op jit(solution)/shard_map/pallas_call | solution.py:290
  165.2 9.4 %shard_map.192 = (f32[32,64,128]{2,1,0:T(8,128)S(1)}, f32[1,128]{1,0:T(1,128)S(1)}) custom-call(s32[256]{0:T(256)S(1)} %fusion.3.refs_0_, f32[32,64,128]{2,1,0:T(8,128)S(1)} %get-tuple-element.36.refs_1_, f32[32,1,128]{2,1,0:T(1,128)S(1)} %get-tuple-element.37.refs_2_, bf16[8,256,256]{2,1,0:T(8,128)(2,1)S(1)} %copy-done.1, ...), custom_call_target="tpu_custom_call" | custom-call | tf_op jit(solution)/shard_map/pallas_call | solution.py:607
  174.6 30.7 %shard_map.193.refs_0_ = f32[32,64,128]{2,1,0:T(8,128)S(1)} custom-call(f32[32,64,128]{2,1,0:T(8,128)S(1)} %get-tuple-element.38.refs_0_), custom_call_target="tpu_custom_call" | custom-call | tf_op jit(solution)/shard_map/pallas_call | solution.py:290
  205.3 2.5 shard_map.194
  207.8 31.0 %shard_map.195 = (f32[32,64,128]{2,1,0:T(8,128)S(1)}, f32[32,1,128]{2,1,0:T(1,128)S(1)}) custom-call(f32[32,64,128]{2,1,0:T(8,128)S(1)} %get-tuple-element.39.refs_0_, f32[32,1,128]{2,1,0:T(1,128)S(1)} %get-tuple-element.40.refs_1_), custom_call_target="tpu_custom_call" | custom-call | tf_op jit(solution)/shard_map/pallas_call | solution.py:290
  238.8 9.4 %shard_map.196 = (f32[32,64,128]{2,1,0:T(8,128)S(1)}, f32[1,128]{1,0:T(1,128)S(1)}) custom-call(s32[256]{0:T(256)S(1)} %fusion.3.refs_0_, f32[32,64,128]{2,1,0:T(8,128)S(1)} %get-tuple-element.41.refs_1_, f32[32,1,128]{2,1,0:T(1,128)S(1)} %get-tuple-element.42.refs_2_, bf16[8,256,256]{2,1,0:T(8,128)(2,1)S(1)} %copy-done.1, ...), custom_call_target="tpu_custom_call" | custom-call | tf_op jit(solution)/shard_map/pallas_call | solution.py:607
  248.2 30.7 %shard_map.197.refs_0_ = f32[32,64,128]{2,1,0:T(8,128)S(1)} custom-call(f32[32,64,128]{2,1,0:T(8,128)S(1)} %get-tuple-element.43.refs_0_), custom_call_target="tpu_custom_call" | custom-call | tf_op jit(solution)/shard_map/pallas_call | solution.py:290
  278.9 1.4 shard_map.198
  280.3 19.1 %shard_map.199 = f32[32,1,128]{2,1,0:T(1,128)S(1)} custom-call(f32[32,1,128]{2,1,0:T(1,128)S(1)} %get-tuple-element.45.refs_0_), custom_call_target="tpu_custom_call" | custom-call | tf_op jit(solution)/shard_map/pallas_call | solution.py:290
  299.4 0.6 slice_reduce_fusion
  300.8 0.6 pad_maximum_fusion
  301.4 0.4 mul.34
  301.9 1.1 copy.29
  (23 shorter events, 0.2 us)
Async XLA Ops:
  0.6 5.8 %copy-start.4 = (f32[32,32,128]{2,1,0:T(8,128)S(1)}, f32[32,32,128]{2,1,0:T(8,128)}, u32[]{:S(2)}) copy-start(f32[32,32,128]{2,1,0:T(8,128)} %constant.81.clone.refs_2_) | copy-start | bytes 1572868
  0.6 5.8 %copy-start.5 = (f32[32,32,128]{2,1,0:T(8,128)S(1)}, f32[32,32,128]{2,1,0:T(8,128)}, u32[]{:S(2)}) copy-start(f32[32,32,128]{2,1,0:T(8,128)} %constant.80.clone.refs_1_) | copy-start | bytes 1572868
  0.7 5.8 %copy-start.9 = (bf16[128,64]{1,0:T(8,128)(2,1)S(1)}, bf16[128,64]{1,0:T(8,128)(2,1)}, u32[]{:S(2)}) copy-start(bf16[128,64]{1,0:T(8,128)(2,1)} %constant.83.clone.refs_4_) | copy-start | bytes 49156
  0.7 5.8 %copy-start.10 = (bf16[128,64]{1,0:T(8,128)(2,1)S(1)}, bf16[128,64]{1,0:T(8,128)(2,1)}, u32[]{:S(2)}) copy-start(bf16[128,64]{1,0:T(8,128)(2,1)} %constant.82.clone.refs_3_) | copy-start | bytes 49156
  7.9 66.5 %copy-start.6 = (bf16[256,256]{1,0:T(8,128)(2,1)S(1)}, bf16[256,256]{1,0:T(8,128)(2,1)}, u32[]{:S(2)}) copy-start(bf16[256,256]{1,0:T(8,128)(2,1)} %constant.88.clone.refs_9_.refs_11_) | copy-start | bytes 393220
  8.0 66.5 %copy-start.7 = (bf16[256,256]{1,0:T(8,128)(2,1)S(1)}, bf16[256,256]{1,0:T(8,128)(2,1)}, u32[]{:S(2)}) copy-start(bf16[256,256]{1,0:T(8,128)(2,1)} %constant.87.clone.refs_8_.refs_10_) | copy-start | bytes 393220
  8.0 66.5 %copy-start.13 = (f32[32,128]{1,0:T(8,128)S(1)}, f32[32,128]{1,0:T(8,128)}, u32[]{:S(2)}) copy-start(f32[32,128]{1,0:T(8,128)} %constant.86.clone.refs_7_) | copy-start | bytes 49156
  8.0 66.5 %copy-start.14 = (f32[32,128]{1,0:T(8,128)S(1)}, f32[32,128]{1,0:T(8,128)}, u32[]{:S(2)}) copy-start(f32[32,128]{1,0:T(8,128)} %constant.85.clone.refs_6_) | copy-start | bytes 49156
  69.6 1.3 copy-start.8
  74.5 1.2 copy-start
  75.7 1.2 copy-start.2
  76.9 54.6 %copy-start.11 = (bf16[64,128]{1,0:T(8,128)(2,1)S(1)}, bf16[64,128]{1,0:T(8,128)(2,1)}, u32[]{:S(2)}) copy-start(bf16[64,128]{1,0:T(8,128)(2,1)} %constant.90.clone.refs_6_.refs_4_) | copy-start | bytes 49156
  77.0 54.6 %copy-start.12 = (bf16[64,128]{1,0:T(8,128)(2,1)S(1)}, bf16[64,128]{1,0:T(8,128)(2,1)}, u32[]{:S(2)}) copy-start(bf16[64,128]{1,0:T(8,128)(2,1)} %constant.89.clone.refs_5_.refs_3_) | copy-start | bytes 49156
  131.6 33.6 %copy-start.1 = (bf16[8,256,256]{2,1,0:T(8,128)(2,1)S(1)}, bf16[8,256,256]{2,1,0:T(8,128)(2,1)}, u32[]{:S(2)}) copy-start(bf16[8,256,256]{2,1,0:T(8,128)(2,1)} %get-tuple-element.31.refs_3_) | copy-start | bytes 3145732
  131.6 33.6 %copy-start.3 = (bf16[8,256,256]{2,1,0:T(8,128)(2,1)S(1)}, bf16[8,256,256]{2,1,0:T(8,128)(2,1)}, u32[]{:S(2)}) copy-start(bf16[8,256,256]{2,1,0:T(8,128)(2,1)} %get-tuple-element.32.refs_4_) | copy-start | bytes 3145732
